TPU v7x, 32 devices: a whole 2x2x4 slice. The times are simulated.
32 devices in a mesh: dp: 4 (over z), row: 2 (over core), col: 4 (over y, x).
Axes of the slice: x: 2, y: 2, z: 4, core: 2. Of those that a mesh axis runs over, the one named last changes fastest.
Arguments:
- hidden_in: bfloat16 [16384, 768], P(('dp', 'row', 'col')), may hold values from -6 to 6
- seq_lengths: int32 [32], P(('dp', 'row')), may hold values from 128 to 512, as said below
- query_weight: bfloat16 [768, 768], P('col', 'row'), may hold values from -0.21875 to 0.21875
- key_weight: bfloat16 [768, 768], P('col', 'row'), may hold values from -0.21875 to 0.21875
- value_weight: bfloat16 [768, 768], P('col', 'row'), may hold values from -0.21875 to 0.21875
- query_bias: float32 [768], P('col'), may hold values from -3 to 3
- value_bias: float32 [768], P('col'), may hold values from -3 to 3
- output_weight: bfloat16 [768, 768], P('col', 'row'), may hold values from -2 to 2
- output_bias: float32 [768], replicated, may hold values from -3 to 3
- first_gain: float32 [768], replicated, may hold values from 0.5 to 1.5
- first_shift: float32 [768], replicated, may hold values from -3 to 3
- inner_weight: bfloat16 [768, 3072], P('row', 'col'), may hold values from -0.21875 to 0.21875
- inner_bias: float32 [3072], P('col'), may hold values from -3 to 3
- outer_weight: bfloat16 [3072, 768], P('col', 'row'), may hold values from -0.109375 to 0.109375
- outer_bias: float32 [768], replicated, may hold values from -3 to 3
- second_gain: float32 [768], replicated, may hold values from 0.5 to 1.5
- second_shift: float32 [768], replicated, may hold values from -3 to 3
- cotangent: bfloat16 [16384, 768], P(('dp', 'row', 'col')), may hold values from -6 to 6
Outputs:
- result: bfloat16 [16384, 768], P(('dp', 'row', 'col'))
- grad_input: float32 [16384, 768], P(('dp', 'row', 'col'))
- grad_query_weight: float32 [768, 768], P('col', 'row')
- grad_key_weight: float32 [768, 768], P('col', 'row')
- grad_value_weight: float32 [768, 768], P('col', 'row')
- grad_query_bias: float32 [768], P('col')
- grad_value_bias: float32 [768], P('col')
- grad_output_weight: float32 [768, 768], P('col', 'row')
- grad_output_bias: float32 [768], replicated
- grad_first_gain: float32 [768], replicated
- grad_first_shift: float32 [768], replicated
- grad_inner_weight: float32 [768, 3072], P('row', 'col')
- grad_inner_bias: float32 [3072], P('col')
- grad_outer_weight: float32 [3072, 768], P('col', 'row')
- grad_outer_bias: float32 [768], replicated
- grad_second_gain: float32 [768], replicated
- grad_second_shift: float32 [768], replicated
Inputs may be any that keep to these rules, and one draw needn't show every extreme that they name: `seq_lengths`: valid tokens of each sequence, counted from its start; in every draw some sequence is full.
All inputs are finite; a program needn't handle non-finite values.
Results may differ from a plain program's by a relative error of at most 0.014.
Values may be sent and summed in bfloat16 or wider, within the bound.
A program may use at most 128 MiB of HBM per device.

v0:
```python
from functools import partial

import jax
import jax.numpy as jnp
from jax import lax
from jax.sharding import PartitionSpec as P

HD = 64


EPSILON = 1e-05


def cols_gather(value):
    return lax.all_gather(value, "col", axis=0, tiled=True)


def cols_reduce(value):
    return lax.psum_scatter(value, "col", scatter_dimension=0, tiled=True)


def dot_plain(left, right):
    return jnp.dot(left, right, preferred_element_type=jnp.float32)


def dot_first(left, right):
    return lax.dot_general(
        left, right, (((0,), (0,)), ((), ())), preferred_element_type=jnp.float32
    )


def dot_second(left, right):
    return lax.dot_general(
        left, right, (((1,), (1,)), ((), ())), preferred_element_type=jnp.float32
    )


def norm_stats(resid):
    center = jnp.mean(resid, axis=1, keepdims=True)
    deviate = resid - center
    spread = jnp.mean(deviate * deviate, axis=1, keepdims=True)
    inverse = lax.rsqrt(spread + EPSILON)
    return (deviate * inverse, inverse)


def norm_backward(grad, scaled, inverse, gain):
    weighted = grad * gain
    first_mean = jnp.mean(weighted, axis=1, keepdims=True)
    second_mean = jnp.mean(weighted * scaled, axis=1, keepdims=True)
    return inverse * (weighted - first_mean - scaled * second_mean)


def score_block(query_heads, key_heads, keep):
    scores = jnp.einsum(
        "sqhd,skhd->shqk", query_heads, key_heads, preferred_element_type=jnp.float32
    ) * HD ** (-0.5)
    return jnp.where(keep, scores, -1e30)


def per_device(
    hidden_in,
    seq_lengths,
    query_weight,
    key_weight,
    value_weight,
    query_bias,
    value_bias,
    output_weight,
    output_bias,
    first_gain,
    first_shift,
    inner_weight,
    inner_bias,
    outer_weight,
    outer_bias,
    second_gain,
    second_shift,
    cotangent,
):
    bf16 = jnp.bfloat16
    query_full, key_full, value_full, output_full, inner_full, outer_full = (
        lax.all_gather(query_weight, "row", axis=1, tiled=True),
        lax.all_gather(key_weight, "row", axis=1, tiled=True),
        lax.all_gather(value_weight, "row", axis=1, tiled=True),
        lax.all_gather(output_weight, "row", axis=1, tiled=True),
        lax.all_gather(inner_weight, "row", axis=0, tiled=True),
        lax.all_gather(outer_weight, "row", axis=1, tiled=True),
    )
    inputs = cols_gather(hidden_in)
    tokens = inputs.shape[0]
    seqs = seq_lengths.shape[0]
    length = tokens // seqs
    heads_here = query_full.shape[0] // HD
    shaped = (seqs, length, heads_here, HD)
    positions = lax.broadcasted_iota(jnp.int32, (seqs, 1, 1, length), 3)
    keep = positions < seq_lengths[:, None, None, None]
    queries = (dot_second(inputs, query_full) + query_bias).astype(bf16)
    keys = dot_second(inputs, key_full).astype(bf16)
    values = (dot_second(inputs, value_full) + value_bias).astype(bf16)
    query_heads = queries.reshape(shaped)
    key_heads = keys.reshape(shaped)
    value_heads = values.reshape(shaped)
    scores = score_block(query_heads, key_heads, keep)
    top = jnp.max(scores, axis=-1, keepdims=True)
    expo = jnp.exp(scores - top)
    total = jnp.sum(expo, axis=-1, keepdims=True)
    probs = expo / total
    log_total = top + jnp.log(total)
    context = (
        jnp.einsum(
            "shqk,skhd->sqhd", probs.astype(bf16), value_heads, preferred_element_type=jnp.float32
        )
        .astype(bf16)
        .reshape(tokens, -1)
    )
    attended = cols_reduce(dot_plain(context, output_full))
    resid_one = attended + output_bias + hidden_in.astype(jnp.float32)
    scaled_one, inverse_one = norm_stats(resid_one)
    normed_one = scaled_one * first_gain + first_shift
    normed_full = cols_gather(normed_one.astype(bf16))
    inner = dot_plain(normed_full, inner_full) + inner_bias
    active, gelu_back = jax.vjp(partial(jax.nn.gelu, approximate=False), inner)
    active_low = active.astype(bf16)
    outer = cols_reduce(dot_plain(active_low, outer_full))
    resid_two = outer + outer_bias + normed_one
    scaled_two, inverse_two = norm_stats(resid_two)
    result = (scaled_two * second_gain + second_shift).astype(bf16)
    grad_out = cotangent.astype(jnp.float32)
    grad_second_gain = jnp.sum(grad_out * scaled_two, axis=0)
    grad_second_shift = jnp.sum(grad_out, axis=0)
    grad_two = norm_backward(grad_out, scaled_two, inverse_two, second_gain)
    grad_outer_bias = jnp.sum(grad_two, axis=0)
    grad_outer_full = cols_gather(grad_two.astype(bf16))
    grad_outer_weight = dot_first(active_low, grad_outer_full)
    grad_active = dot_second(grad_outer_full, outer_full)
    grad_inner = gelu_back(grad_active)[0].astype(bf16)
    grad_inner_bias = jnp.sum(grad_inner.astype(jnp.float32), axis=0)
    grad_inner_weight = dot_first(normed_full, grad_inner)
    grad_one = cols_reduce(dot_second(grad_inner, inner_full)) + grad_two
    grad_first_gain = jnp.sum(grad_one * scaled_one, axis=0)
    grad_first_shift = jnp.sum(grad_one, axis=0)
    grad_resid = norm_backward(grad_one, scaled_one, inverse_one, first_gain)
    grad_output_bias = jnp.sum(grad_resid, axis=0)
    grad_attn_full = cols_gather(grad_resid.astype(bf16))
    grad_output_weight = dot_first(context, grad_attn_full)
    grad_context = dot_second(grad_attn_full, output_full).astype(bf16).reshape(shaped)
    scores_again = score_block(query_heads, key_heads, keep)
    probs_again = jnp.exp(scores_again - log_total)
    probs_low = probs_again.astype(bf16)
    grad_probs = jnp.einsum(
        "sqhd,skhd->shqk", grad_context, value_heads, preferred_element_type=jnp.float32
    )
    row_dot = jnp.sum(probs_again * grad_probs, axis=-1, keepdims=True)
    grad_scores = (probs_again * (grad_probs - row_dot)).astype(bf16)
    grad_queries = (
        (
            jnp.einsum(
                "shqk,skhd->sqhd", grad_scores, key_heads, preferred_element_type=jnp.float32
            )
            * HD ** (-0.5)
        )
        .astype(bf16)
        .reshape(tokens, -1)
    )
    grad_keys = (
        (
            jnp.einsum(
                "shqk,sqhd->skhd", grad_scores, query_heads, preferred_element_type=jnp.float32
            )
            * HD ** (-0.5)
        )
        .astype(bf16)
        .reshape(tokens, -1)
    )
    grad_values = (
        jnp.einsum("shqk,sqhd->skhd", probs_low, grad_context, preferred_element_type=jnp.float32)
        .astype(bf16)
        .reshape(tokens, -1)
    )
    grad_query_bias = jnp.sum(grad_queries.astype(jnp.float32), axis=0)
    grad_value_bias = jnp.sum(grad_values.astype(jnp.float32), axis=0)
    grad_query_weight = dot_first(grad_queries, inputs)
    grad_key_weight = dot_first(grad_keys, inputs)
    grad_value_weight = dot_first(grad_values, inputs)
    input_terms = (
        dot_plain(grad_queries, query_full)
        + dot_plain(grad_keys, key_full)
        + dot_plain(grad_values, value_full)
    )
    grad_input = cols_reduce(input_terms) + grad_resid
    norm_sums = lax.psum(
        (
            grad_output_bias,
            grad_first_gain,
            grad_first_shift,
            grad_outer_bias,
            grad_second_gain,
            grad_second_shift,
        ),
        ("dp", "row", "col"),
    )
    summed = lax.psum(
        (
            grad_query_weight,
            grad_key_weight,
            grad_value_weight,
            grad_output_weight,
            grad_inner_weight,
            grad_outer_weight,
            grad_query_bias,
            grad_value_bias,
            grad_inner_bias,
        ),
        ("dp", "row"),
    )
    rank = lax.axis_index("row")
    pieces = lax.axis_size("row")

    def own_block(value, dim):
        width = value.shape[dim] // pieces
        return lax.dynamic_slice_in_dim(value, rank * width, width, dim)

    weight_query = own_block(summed[0], 1)
    weight_key = own_block(summed[1], 1)
    weight_value = own_block(summed[2], 1)
    weight_output = own_block(summed[3], 1)
    weight_inner = own_block(summed[4], 0)
    weight_outer = own_block(summed[5], 1)
    head_sums = summed[6:]
    return (
        result,
        grad_input,
        weight_query,
        weight_key,
        weight_value,
        head_sums[0],
        head_sums[1],
        weight_output,
        norm_sums[0],
        norm_sums[1],
        norm_sums[2],
        weight_inner,
        head_sums[2],
        weight_outer,
        norm_sums[3],
        norm_sums[4],
        norm_sums[5],
    )


def solution(mesh):
    in_specs = (
        P(("dp", "row", "col"), None),
        P(("dp", "row")),
        P("col", "row"),
        P("col", "row"),
        P("col", "row"),
        P("col"),
        P("col"),
        P("col", "row"),
        P(),
        P(),
        P(),
        P("row", "col"),
        P("col"),
        P("col", "row"),
        P(),
        P(),
        P(),
        P(("dp", "row", "col"), None),
    )
    out_specs = (
        P(("dp", "row", "col"), None),
        P(("dp", "row", "col"), None),
        P("col", "row"),
        P("col", "row"),
        P("col", "row"),
        P("col"),
        P("col"),
        P("col", "row"),
        P(),
        P(),
        P(),
        P("row", "col"),
        P("col"),
        P("col", "row"),
        P(),
        P(),
        P(),
    )
    return jax.shard_map(
        per_device, mesh=mesh, in_specs=in_specs, out_specs=out_specs, check_vma=False
    )
```

profile of v0, /device:TPU:0, one launch (start us, length us, event | category | flops | bytes accessed | tf_op | source)
XLA Modules:
  0.0 769.4 jit_solution(6650983520701413565)
XLA Ops:
  8.8 4.0 all_gather.32
  12.8 2.3 all_gather.33
  15.1 3.7 all_gather.31
  18.8 3.9 all_gather.34
  23.3 34.1 %all-gather.7.cloned.1.call-done = bf16[2048,768]{1,0:T(8,128)(2,1)} async-done(((bf16[512,768]{1,0:T(8,128)(2,1)}), bf16[2048,768]{1,0:T(8,128)(2,1)}) %all-gather.7.cloned.1.call-update) | async-done | bytes 3145744 | tf_op jit(solution)/shard_map/all_gather | solution.py:15
  57.4 4.2 fusion.13
  61.6 3.0 reshape.138
  64.6 2.1 convolution_convert_fusion.1
  66.6 3.0 reshape.140
  69.6 3.0 fusion.14
  72.6 2.3 reshape.139
  74.9 4.5 fusion.12
  79.5 3.6 fusion
  83.1 0.9 copy-done
  84.0 3.8 fusion.32
  89.5 3.6 fusion.53
  93.8 11.7 %all-gather.9.cloned.1.call-start = ((), (), s32[]{:S(2)}) async-start(), calls=%async_computation.6 | async-start | bytes 3932160 | tf_op jit(solution)/shard_map/all_gather | solution.py:15
  105.5 58.0 %reduce-scatter.5.cloned.1.call-done = f32[512,768]{1,0:T(8,128)} async-done(((f32[2048,768]{1,0:T(8,128)}), f32[512,768]{1,0:T(8,128)}) %reduce-scatter.5.cloned.1.call-update) | async-done | bytes 1572880 | tf_op jit(solution)/shard_map/reduce_scatter | solution.py:19
  163.5 1.7 fusion.52
  165.6 1.2 fusion.26
  167.4 43.3 %all-gather.9.cloned.1.call-done = bf16[2048,768]{1,0:T(8,128)(2,1)} async-done(((bf16[512,768]{1,0:T(8,128)(2,1)}), bf16[2048,768]{1,0:T(8,128)(2,1)}) %all-gather.9.cloned.1.call-update) | async-done | bytes 3145744 | tf_op jit(solution)/shard_map/all_gather | solution.py:15
  210.7 19.0 %multiply_convert_fusion.1 = (bf16[2048,768]{1,0:T(8,128)(2,1)}, f32[2048,768]{1,0:T(8,128)}, f32[2048,768]{1,0:T(8,128)}) fusion(f32[768]{0:T(1024)S(1)} %copy-done.31, bf16[2048,768]{1,0:T(8,128)(2,1)} %all-gather.9.cloned.1.call-done, bf16[768,768]{1,0:T(8,128)(2,1)} %all-gather.11.cloned.1.call-done), kind=kOutput, calls=%fused_computation.15 | convolution fusion | flops 2519728128 | bytes 20057088 | tf_op jit(solution)/shard_map/dot_general | solution.py:23
  229.7 7.5 fusion.54
  237.3 70.1 %reduce-scatter.7.cloned.1.call-done = f32[512,768]{1,0:T(8,128)} async-done(((f32[2048,768]{1,0:T(8,128)}), f32[512,768]{1,0:T(8,128)}) %reduce-scatter.7.cloned.1.call-update) | async-done | bytes 1572880 | tf_op jit(solution)/shard_map/reduce_scatter | solution.py:19
  307.4 2.0 fusion.50
  310.5 1.5 fusion.47
  312.1 1.0 convert_element_type.91
  313.1 44.1 %all-gather.15.cloned.1.call-done = bf16[2048,768]{1,0:T(8,128)(2,1)} async-done(((bf16[512,768]{1,0:T(8,128)(2,1)}), bf16[2048,768]{1,0:T(8,128)(2,1)}) %all-gather.15.cloned.1.call-update) | async-done | bytes 3145744 | tf_op jit(solution)/shard_map/all_gather | solution.py:15
  357.2 10.6 %convert_reduce_fusion = (f32[768]{0:T(1024)S(1)}, bf16[2048,768]{1,0:T(8,128)(2,1)S(1)}) fusion(f32[2048,768]{1,0:T(8,128)} %get-tuple-element.50, f32[2048,768]{1,0:T(8,128)} %get-tuple-element.56, f32[768]{0:T(1024)S(1)} %copy-done.31, bf16[2048,768]{1,0:T(8,128)(2,1)} %all-gather.15.cloned.1.call-done, bf16[768,768]{1,0:T(8,128)(2,1)} %all-gather.13.cloned.1.call-done), kind=kOutput, calls=%fused_computation.11 | convolution fusion | flops 2442657024 | bytes 20060160 | tf_op jit(solution)/shard_map/dot_general | solution.py:33
  367.8 1.7 copy-done.33
  369.5 4.5 fusion.55
  374.1 70.1 %reduce-scatter.9.cloned.1.call-done = f32[512,768]{1,0:T(8,128)} async-done(((f32[2048,768]{1,0:T(8,128)}), f32[512,768]{1,0:T(8,128)}) %reduce-scatter.9.cloned.1.call-update) | async-done | bytes 1572880 | tf_op jit(solution)/shard_map/reduce_scatter | solution.py:19
  444.2 2.3 multiply_reduce_fusion.1
  447.0 1.1 copy-done.3
  448.1 1.0 convert_element_type.93
  449.6 7.1 fusion.63
  456.7 4.2 fusion.62
  460.9 32.4 %all-gather.17.cloned.1.call-done = bf16[2048,768]{1,0:T(8,128)(2,1)} async-done(((bf16[512,768]{1,0:T(8,128)(2,1)}), bf16[2048,768]{1,0:T(8,128)(2,1)}) %all-gather.17.cloned.1.call-update) | async-done | bytes 3145744 | tf_op jit(solution)/shard_map/all_gather | solution.py:15
  493.2 3.1 convolution_convert_fusion
  496.9 0.9 copy-done.11
  497.8 8.2 %convert_reduce_fusion.2 = (f32[3,64]{1,0:T(4,128)S(1)}, bf16[4,512,3,64]{1,3,2,0:T(8,128)(2,1)}) fusion(f32[4,3,512]{2,1,0:T(4,128)S(1)} %log_add_fusion, f32[4,3,512,512]{2,3,1,0:T(8,128)} %copy-done, pred[4,512]{1,0:T(4,128)(4,1)S(1)} %iota_compare_fusion, bf16[4,512,3,64]{1,0,3,2:T(4,128)(2,1)S(1)} %reshape.142), kind=kOutput, calls=%fused_computation.48 | convolution fusion | flops 416415552 | bytes 14183168 | tf_op jit(solution)/shard_map/shqk,sqhd->skhd/dot_general | solution.py:176
  506.0 8.1 %multiply_reduce_fusion = (f32[4,3,512]{2,1,0:T(4,128)S(1)}, f32[4,3,512,512]{2,3,1,0:T(8,128)S(1)}) fusion(f32[4,3,512]{2,1,0:T(4,128)S(1)} %log_add_fusion, f32[4,3,512,512]{2,3,1,0:T(8,128)} %copy-done, pred[4,512]{1,0:T(4,128)(4,1)S(1)} %iota_compare_fusion, bf16[4,512,3,64]{1,0,3,2:T(4,128)(2,1)} %reshape.138, bf16[4,512,3,64]{1,0,3,2:T(4,128)(2,1)} %copy-done.11), kind=kOutput, calls=%fused_computation.1 | convolution fusion | flops 418375680 | bytes 26789888 | tf_op jit(solution)/shard_map/sqhd,skhd->shqk/dot_general | solution.py:150
  514.1 4.3 multiply_convert_fusion
  518.4 2.0 fusion.31
  520.5 1.2 convert_reduce_fusion.3
  524.7 1.7 fusion.61
  526.3 1.6 fusion.60
  527.9 1.6 fusion.59
  529.5 1.6 fusion.58
  531.2 0.9 copy-done.18
  532.1 1.0 fusion.56
  533.1 1.0 fusion.57
  534.2 3.9 add_add_fusion
  538.1 41.5 %all-reduce = (f32[768]{0:T(1024)}, f32[768]{0:T(1024)}, f32[768]{0:T(1024)}, f32[768]{0:T(1024)}, f32[768]{0:T(1024)}, /*index=5*/f32[768]{0:T(1024)}) all-reduce(f32[768]{0:T(1024)S(1)} %get-tuple-element.42, f32[768]{0:T(1024)S(1)} %get-tuple-element.17, ...), channel_id=1, replica_groups=mesh['dp'=4,'row'=2,'col'=4] {'dp','row','col'}, use_global_device_ids=true, to_apply=%region_24.25 | all-reduce | flops 4608 | bytes 36864 | tf_op jit(solution)/shard_map/psum | solution.py:191
  579.8 17.8 %all-reduce.1 = (f32[192]{0:T(256)}, f32[192]{0:T(256)}, f32[768]{0:T(1024)}) all-reduce(f32[192]{0:T(256)S(1)} %reduce_sum.186, f32[192]{0:T(256)S(1)} %reduce_sum.188, f32[768]{0:T(1024)S(1)} %get-tuple-element.44), channel_id=1, replica_groups=mesh['dp'=4,'row'=2,'col'=4] {'dp','row'}, use_global_device_ids=true, to_apply=%region_19.20 | all-reduce | flops 1152 | bytes 9216 | tf_op jit(solution)/shard_map/psum | solution.py:202
  597.6 88.1 %all-reduce.5.cloned.1.call-done = (f32[192,768]{1,0:T(8,128)}, f32[192,768]{1,0:T(8,128)}, f32[192,768]{1,0:T(8,128)}, f32[192,768]{1,0:T(8,128)}, f32[768,768]{1,0:T(8,128)}, /*index=5*/f32[768,768]{1,0:T(8,128)}) async-done(((f32[192,768]{1,0:T(8,128)}, f32[192,768]{1,0:T(8,128)}, f32[192,768]{1,0:T(8,128)}, f32[192,768]{1,0:T(8,128)}, f32[768,768]{1,0:T(8,128)}, /*index=5*/f32[768,768]{1,0:T(8,128)}), ...) | async-done | bytes 7077904 | tf_op jit(solution)/shard_map/psum | solution.py:202
  685.6 1.8 constant_dynamic-slice_fusion.5
  687.5 1.8 constant_dynamic-slice_fusion.4
  689.3 1.7 constant_dynamic-slice_fusion.3
  691.0 1.7 constant_dynamic-slice_fusion.2
  692.7 2.4 constant_dynamic-slice_fusion.1
  695.1 1.1 constant_dynamic-slice_fusion
  696.1 62.7 %reduce-scatter.11.cloned.1.call-done = f32[512,768]{1,0:T(8,128)} async-done(((f32[2048,768]{1,0:T(8,128)}), f32[512,768]{1,0:T(8,128)}) %reduce-scatter.11.cloned.1.call-update) | async-done | bytes 1572880 | tf_op jit(solution)/shard_map/reduce_scatter | solution.py:19
  758.9 2.7 add.166
  (119 shorter events, 10.8 us)
Async XLA Ops:
  8.0 49.4 %all-gather.7.cloned.1.call-start = ((), (), s32[]{:S(2)}) async-start(), calls=%async_computation.4 | async-start | bytes 3932160 | tf_op jit(solution)/shard_map/all_gather | solution.py:15
  8.8 154.8 %reduce-scatter.5.cloned.1.call-start = ((), (), s32[]{:S(2)}) async-start(), calls=%async_computation.5 | async-start | bytes 7864320 | tf_op jit(solution)/shard_map/reduce_scatter | solution.py:19
  15.1 49.5 %copy-start.16 = (bf16[192,768]{1,0:T(8,128)(2,1)}, bf16[192,768]{1,0:T(8,128)(2,1)S(1)}, u32[]{:S(2)}) copy-start(bf16[192,768]{1,0:T(8,128)(2,1)S(1)} %all_gather.33) | copy-start | bytes 884740
  57.4 7.2 copy-start.1
  64.6 5.0 copy-start.32
  74.9 4.5 copy-start.5
  79.5 4.5 copy-start
  79.5 4.5 copy-start.10
  87.8 1.7 copy-start.19
  88.6 0.9 copy-start.7
  93.1 70.4 %copy-start.13 = (bf16[512,768]{1,0:T(8,128)(2,1)S(1)}, bf16[512,768]{1,0:T(8,128)(2,1)}, u32[]{:S(2)}) copy-start(bf16[512,768]{1,0:T(8,128)(2,1)} %param.18) | copy-start | bytes 2359300
  93.1 70.4 %copy-start.26 = (f32[768]{0:T(1024)S(1)}, f32[768]{0:T(1024)}, u32[]{:S(2)}) copy-start(f32[768]{0:T(1024)} %param.26) | copy-start | bytes 9220
  93.2 72.4 %copy-start.23 = (f32[768]{0:T(1024)S(1)}, f32[768]{0:T(1024)}, u32[]{:S(2)}) copy-start(f32[768]{0:T(1024)} %param.27) | copy-start | bytes 9220
  93.2 72.4 %copy-start.24 = (f32[768]{0:T(1024)S(1)}, f32[768]{0:T(1024)}, u32[]{:S(2)}) copy-start(f32[768]{0:T(1024)} %param.28) | copy-start | bytes 9220
  93.2 74.3 %all-gather.11.cloned.1.call-start = ((), (), s32[]{:S(2)}) async-start(), calls=%async_computation.7 | async-start | bytes 1769472 | tf_op jit(solution)/shard_map/all_gather | solution.py:86
  93.8 116.9 %all-gather.9.cloned.1.call-start = ((), (), s32[]{:S(2)}) async-start(), calls=%async_computation.6 | async-start | bytes 3932160 | tf_op jit(solution)/shard_map/all_gather | solution.py:15
  165.2 45.5 %copy-start.31 = (f32[768]{0:T(1024)S(1)}, f32[768]{0:T(1024)}, u32[]{:S(2)}) copy-start(f32[768]{0:T(1024)} %param.30) | copy-start | bytes 9220
  166.8 62.9 %all-gather.13.cloned.1.call-start = ((), (), s32[]{:S(2)}) async-start(), calls=%async_computation.8 | async-start | bytes 1769472 | tf_op jit(solution)/shard_map/all_gather | solution.py:87
  167.4 140.0 %reduce-scatter.7.cloned.1.call-start = ((), (), s32[]{:S(2)}) async-start(), calls=%async_computation.9 | async-start | bytes 7864320 | tf_op jit(solution)/shard_map/reduce_scatter | solution.py:19
  237.2 70.2 %copy-start.27 = (f32[768]{0:T(1024)S(1)}, f32[768]{0:T(1024)}, u32[]{:S(2)}) copy-start(f32[768]{0:T(1024)} %param.32) | copy-start | bytes 9220
  237.2 72.5 %copy-start.14 = (bf16[512,768]{1,0:T(8,128)(2,1)S(1)}, bf16[512,768]{1,0:T(8,128)(2,1)}, u32[]{:S(2)}) copy-start(bf16[512,768]{1,0:T(8,128)(2,1)} %param.35) | copy-start | bytes 2359300
  237.2 72.5 %copy-start.25 = (f32[768]{0:T(1024)S(1)}, f32[768]{0:T(1024)}, u32[]{:S(2)}) copy-start(f32[768]{0:T(1024)} %param.33) | copy-start | bytes 9220
  237.3 119.9 %all-gather.15.cloned.1.call-start = ((), (), s32[]{:S(2)}) async-start(), calls=%async_computation.10 | async-start | bytes 3932160 | tf_op jit(solution)/shard_map/all_gather | solution.py:15
  309.4 1.2 copy-start.15
  309.4 1.2 copy-start.28
  313.1 131.1 %reduce-scatter.9.cloned.1.call-start = ((), (), s32[]{:S(2)}) async-start(), calls=%async_computation.11 | async-start | bytes 7864320 | tf_op jit(solution)/shard_map/reduce_scatter | solution.py:19
  357.2 12.3 %copy-start.30 = (bf16[768,768]{1,0:T(8,128)(2,1)S(1)}, bf16[768,768]{1,0:T(8,128)(2,1)}, u32[]{:S(2)}) copy-start(bf16[768,768]{1,0:T(8,128)(2,1)} %all-gather.11.cloned.1.call-done) | copy-start | bytes 3538948
  367.8 1.7 copy-start.33
  374.0 119.2 %all-gather.17.cloned.1.call-start = ((), (), s32[]{:S(2)}) async-start(), calls=%async_computation.12 | async-start | bytes 3932160 | tf_op jit(solution)/shard_map/all_gather | solution.py:15
  447.0 1.1 copy-start.3
  449.1 236.6 %all-reduce.5.cloned.1.call-start = ((), (), s32[]{:S(2)}) async-start(), calls=%async_computation.14 | async-start | bytes 14155776 | tf_op jit(solution)/shard_map/psum | solution.py:202
  449.6 7.1 copy-start.29
  449.6 7.1 copy-start.34
  496.9 0.9 copy-start.11
  497.8 16.3 %slice-start = ((s8[12582912]{0:T(1024)(128)(4,1)}), s8[4194304]{0:T(1024)(128)(4,1)S(1)}, s32[]{:S(2)}) async-start(s8[12582912]{0:T(1024)(128)(4,1)} %bitcast.74), calls=%async_computation.15 | async-start | bytes 8388608
  497.8 16.3 %slice-start.1 = ((s8[12582912]{0:T(1024)(128)(4,1)}), s8[4194304]{0:T(1024)(128)(4,1)S(1)}, s32[]{:S(2)}) async-start(s8[12582912]{0:T(1024)(128)(4,1)} %bitcast.74), calls=%async_computation.16 | async-start | bytes 8388608
  506.0 8.1 %slice-start.2 = ((s8[12582912]{0:T(1024)(128)(4,1)}), s8[4194304]{0:T(1024)(128)(4,1)S(1)}, s32[]{:S(2)}) async-start(s8[12582912]{0:T(1024)(128)(4,1)} %bitcast.74), calls=%async_computation.17 | async-start | bytes 8388608
  514.1 4.4 copy-start.6
  518.4 2.0 copy-start.9
  520.5 1.2 copy-start.21
  522.5 1.6 copy-start.8
  522.5 2.1 copy-start.12
  524.0 2.4 copy-start.2
  531.1 1.0 copy-start.18
  531.1 2.0 copy-start.17
  531.2 227.7 %reduce-scatter.11.cloned.1.call-start = ((), (), s32[]{:S(2)}) async-start(), calls=%async_computation.13 | async-start | bytes 7864320 | tf_op jit(solution)/shard_map/reduce_scatter | solution.py:19
  533.1 1.1 copy-start.20
  685.6 9.4 %copy-start.22 = (f32[768,768]{1,0:T(8,128)S(1)}, f32[768,768]{1,0:T(8,128)}, u32[]{:S(2)}) copy-start(f32[768,768]{1,0:T(8,128)} %get-tuple-element.39) | copy-start | bytes 7077892
  687.5 71.4 %copy-start.4 = (f32[512,768]{1,0:T(8,128)S(1)}, f32[512,768]{1,0:T(8,128)}, u32[]{:S(2)}) copy-start(f32[512,768]{1,0:T(8,128)} %copy-done.3) | copy-start | bytes 4718596
Sparse Core Ops, SparseCore 0:
  10.7 46.6 all-gather.6
  93.3 70.2 reduce-scatter.4
  313.2 43.9 all-gather.14
  449.2 43.9 all-gather.16
  531.3 154.3 all-reduce.4
  688.5 70.3 reduce-scatter.10
Sparse Core Ops, SparseCore 1:
  95.2 9.1 all-gather.10
  166.9 43.8 all-gather.8
  212.1 9.1 all-gather.12
  237.3 70.0 reduce-scatter.6
  374.1 70.0 reduce-scatter.8
where the time goes:
time: 779 us; the launch traced here: 769 us
  waiting for transfers between devices  505 us (65%)
  matrix products  109 us (14%)
  blocking collectives  73.1 us (9%)
  local copies, waits for them, and re-layouts  29.7 us (4%)
  other arithmetic  23.9 us (3%)
  between operations  16.5 us (2%)
  starting transfers between devices  12.6 us (2%)
    reduce_scatter x4, waiting for transfers between devices, cols_reduce(): return lax.psum_scatter(value, 'col', scatter_dimension=0, tiled=True)  261 us
    all_gather x4, waiting for transfers between devices, cols_gather(): return lax.all_gather(value, 'col', axis=0, tiled=True)  154 us
    psum x1, waiting for transfers between devices, per_device(): lax.psum((grad_query_weight, grad_key_weight, grad_value_weight, grad_out...  88.1 us
    psum x1, blocking collectives, per_device(): lax.psum((grad_output_bias, grad_first_gain, grad_first_shift, grad_outer...  41.5 us
    dot_general x6, matrix products, dot_plain(): return jnp.dot(left, right, preferred_element_type=jnp.float32)  36.1 us
    dot_general x6, matrix products, dot_second(): lax.dot_general(left, right, (((1,), (1,)), ((), ())), preferred_element_...  27.3 us
    psum x1, blocking collectives, per_device(): lax.psum((grad_query_weight, grad_key_weight, grad_value_weight, grad_out...  17.8 us
    dot_general x6, matrix products, dot_first(): lax.dot_general(left, right, (((0,), (0,)), ((), ())), preferred_element_...  17.7 us
  transfers between devices with their start and end apart: 11, of which 9 were waited for; matrix products, arithmetic and copies ran while one was open for 7% of the time, Pallas kernels for 0%

commit v1 on v0

v1 whole, which is shorter than its diff:
```python
from functools import partial

import jax
import jax.numpy as jnp
from jax import lax
from jax.sharding import PartitionSpec as P

HD = 64


EPSILON = 1e-05


def gather_blocks(block):
    pieces = lax.all_gather(block, "col", axis=0, tiled=False)
    return lax.all_gather(pieces, "row", axis=0, tiled=False)


def scatter_blocks(parts):
    halves = lax.psum_scatter(parts, "row", scatter_dimension=0, tiled=False)
    own = lax.psum_scatter(halves, "col", scatter_dimension=0, tiled=False)
    return lax.psum(own, "dp")


def split_blocks(value, first, second):
    rows, columns = value.shape
    shaped = value.reshape(first, rows // first, second, columns // second)
    return shaped.transpose(0, 2, 1, 3)


def dot_plain(left, right):
    return jnp.dot(left, right, preferred_element_type=jnp.float32)


def dot_first(left, right):
    return lax.dot_general(
        left, right, (((0,), (0,)), ((), ())), preferred_element_type=jnp.float32
    )


def dot_second(left, right):
    return lax.dot_general(
        left, right, (((1,), (1,)), ((), ())), preferred_element_type=jnp.float32
    )


def norm_stats(resid):
    center = jnp.mean(resid, axis=1, keepdims=True)
    deviate = resid - center
    spread = jnp.mean(deviate * deviate, axis=1, keepdims=True)
    inverse = lax.rsqrt(spread + EPSILON)
    return (deviate * inverse, inverse)


def norm_backward(grad, scaled, inverse, gain):
    weighted = grad * gain
    first_mean = jnp.mean(weighted, axis=1, keepdims=True)
    second_mean = jnp.mean(weighted * scaled, axis=1, keepdims=True)
    return inverse * (weighted - first_mean - scaled * second_mean)


def per_device(
    hidden_in,
    seq_lengths,
    query_weight,
    key_weight,
    value_weight,
    query_bias,
    value_bias,
    output_weight,
    output_bias,
    first_gain,
    first_shift,
    inner_weight,
    inner_bias,
    outer_weight,
    outer_bias,
    second_gain,
    second_shift,
    cotangent,
):
    bf16 = jnp.bfloat16
    f32 = jnp.float32
    row_size, col_size = lax.axis_size("row"), lax.axis_size("col")
    col_rank = lax.axis_index("col")
    small = gather_blocks(jnp.stack([query_weight, key_weight, value_weight, output_weight]))
    small = small.transpose(2, 1, 3, 0, 4).reshape(4, small.shape[3] * col_size, -1)
    query_full, key_full, value_full, output_full = (small[i] for i in range(4))
    inner_full = gather_blocks(inner_weight).transpose(0, 2, 1, 3)
    inner_full = inner_full.reshape(hidden_in.shape[1], -1)
    outer_full = gather_blocks(outer_weight).transpose(1, 2, 0, 3)
    outer_full = outer_full.reshape(-1, hidden_in.shape[1])
    biases = lax.all_gather(
        jnp.concatenate([query_bias, value_bias, inner_bias]), "col", axis=0, tiled=False
    )
    width = query_bias.shape[0]
    query_bias_full = biases[:, :width].reshape(-1)
    value_bias_full = biases[:, width : 2 * width].reshape(-1)
    inner_bias_full = biases[:, 2 * width :].reshape(-1)

    tokens = hidden_in.shape[0]
    seqs = seq_lengths.shape[0] // col_size
    length = tokens // seqs
    heads = query_full.shape[0] // HD
    shaped = (seqs, length, heads, HD)
    own_lengths = lax.dynamic_slice_in_dim(seq_lengths, col_rank * seqs, seqs, 0)
    positions = lax.broadcasted_iota(jnp.int32, (seqs, 1, 1, length), 3)
    keep = positions < own_lengths[:, None, None, None]
    inputs = hidden_in
    queries = (dot_second(inputs, query_full) + query_bias_full).astype(bf16)
    keys = dot_second(inputs, key_full).astype(bf16)
    values = (dot_second(inputs, value_full) + value_bias_full).astype(bf16)
    query_heads = queries.reshape(shaped)
    key_heads = keys.reshape(shaped)
    value_heads = values.reshape(shaped)
    scores = jnp.einsum(
        "sqhd,skhd->shqk", query_heads, key_heads, preferred_element_type=f32
    ) * HD ** (-0.5)
    scores = jnp.where(keep, scores, -1e30)
    top = jnp.max(scores, axis=-1, keepdims=True)
    expo = jnp.exp(scores - top)
    probs = expo / jnp.sum(expo, axis=-1, keepdims=True)
    probs_low = probs.astype(bf16)
    context = (
        jnp.einsum("shqk,skhd->sqhd", probs_low, value_heads, preferred_element_type=f32)
        .astype(bf16)
        .reshape(tokens, -1)
    )
    resid_one = dot_plain(context, output_full) + output_bias + hidden_in.astype(f32)
    scaled_one, inverse_one = norm_stats(resid_one)
    normed_one = scaled_one * first_gain + first_shift
    normed_low = normed_one.astype(bf16)
    inner = dot_plain(normed_low, inner_full) + inner_bias_full
    active, gelu_back = jax.vjp(partial(jax.nn.gelu, approximate=False), inner)
    active_low = active.astype(bf16)
    resid_two = dot_plain(active_low, outer_full) + outer_bias + normed_one
    scaled_two, inverse_two = norm_stats(resid_two)
    result = (scaled_two * second_gain + second_shift).astype(bf16)
    grad_out = cotangent.astype(f32)
    grad_second_gain = jnp.sum(grad_out * scaled_two, axis=0)
    grad_second_shift = jnp.sum(grad_out, axis=0)
    grad_two = norm_backward(grad_out, scaled_two, inverse_two, second_gain)
    grad_outer_bias = jnp.sum(grad_two, axis=0)
    grad_outer_low = grad_two.astype(bf16)
    grad_outer_weight = dot_first(active_low, grad_outer_low).astype(bf16)
    outer_own = scatter_blocks(split_blocks(grad_outer_weight, col_size, row_size).transpose(1, 0, 2, 3))
    grad_active = dot_second(grad_outer_low, outer_full)
    grad_inner = gelu_back(grad_active)[0].astype(bf16)
    grad_inner_bias = jnp.sum(grad_inner.astype(f32), axis=0)
    grad_inner_weight = dot_first(normed_low, grad_inner).astype(bf16)
    inner_own = scatter_blocks(split_blocks(grad_inner_weight, row_size, col_size))
    grad_one = dot_second(grad_inner, inner_full) + grad_two
    grad_first_gain = jnp.sum(grad_one * scaled_one, axis=0)
    grad_first_shift = jnp.sum(grad_one, axis=0)
    grad_resid = norm_backward(grad_one, scaled_one, inverse_one, first_gain)
    grad_output_bias = jnp.sum(grad_resid, axis=0)
    grad_attn_low = grad_resid.astype(bf16)
    grad_output_weight = dot_first(context, grad_attn_low)
    grad_context = dot_second(grad_attn_low, output_full).astype(bf16).reshape(shaped)
    grad_probs = jnp.einsum(
        "sqhd,skhd->shqk", grad_context, value_heads, preferred_element_type=f32
    )
    row_dot = jnp.sum(probs * grad_probs, axis=-1, keepdims=True)
    grad_scores = (probs * (grad_probs - row_dot)).astype(bf16)
    grad_queries = jnp.einsum(
        "shqk,skhd->sqhd", grad_scores, key_heads, preferred_element_type=f32
    ) * HD ** (-0.5)
    grad_queries = grad_queries.astype(bf16).reshape(tokens, -1)
    grad_keys = jnp.einsum(
        "shqk,sqhd->skhd", grad_scores, query_heads, preferred_element_type=f32
    ) * HD ** (-0.5)
    grad_keys = grad_keys.astype(bf16).reshape(tokens, -1)
    grad_values = jnp.einsum(
        "shqk,sqhd->skhd", probs_low, grad_context, preferred_element_type=f32
    )
    grad_values = grad_values.astype(bf16).reshape(tokens, -1)
    grad_query_bias = jnp.sum(grad_queries.astype(f32), axis=0)
    grad_value_bias = jnp.sum(grad_values.astype(f32), axis=0)
    small_grads = jnp.stack(
        [
            split_blocks(value.astype(bf16), col_size, row_size)
            for value in (
                dot_first(grad_queries, inputs),
                dot_first(grad_keys, inputs),
                dot_first(grad_values, inputs),
                grad_output_weight,
            )
        ],
        axis=2,
    )
    small_own = scatter_blocks(small_grads.transpose(1, 0, 2, 3, 4)).astype(f32)
    grad_input = (
        dot_plain(grad_queries, query_full)
        + dot_plain(grad_keys, key_full)
        + dot_plain(grad_values, value_full)
    ) + grad_resid
    parts = (
        grad_output_bias,
        grad_first_gain,
        grad_first_shift,
        grad_outer_bias,
        grad_second_gain,
        grad_second_shift,
        grad_query_bias,
        grad_value_bias,
        grad_inner_bias,
    )
    sums = lax.psum(jnp.concatenate(parts), ("dp", "row", "col"))
    offset, vectors = 0, []
    for part in parts:
        vectors.append(sums[offset : offset + part.shape[0]])
        offset += part.shape[0]

    def own_part(value):
        size = value.shape[0] // col_size
        return lax.dynamic_slice_in_dim(value, col_rank * size, size, 0)

    return (
        result,
        grad_input,
        small_own[0],
        small_own[1],
        small_own[2],
        own_part(vectors[6]),
        own_part(vectors[7]),
        small_own[3],
        vectors[0],
        vectors[1],
        vectors[2],
        inner_own.astype(f32),
        own_part(vectors[8]),
        outer_own.astype(f32),
        vectors[3],
        vectors[4],
        vectors[5],
    )


def solution(mesh):
    in_specs = (
        P(("dp", "row", "col"), None),
        P(("dp", "row")),
        P("col", "row"),
        P("col", "row"),
        P("col", "row"),
        P("col"),
        P("col"),
        P("col", "row"),
        P(),
        P(),
        P(),
        P("row", "col"),
        P("col"),
        P("col", "row"),
        P(),
        P(),
        P(),
        P(("dp", "row", "col"), None),
    )
    out_specs = (
        P(("dp", "row", "col"), None),
        P(("dp", "row", "col"), None),
        P("col", "row"),
        P("col", "row"),
        P("col", "row"),
        P("col"),
        P("col"),
        P("col", "row"),
        P(),
        P(),
        P(),
        P("row", "col"),
        P("col"),
        P("col", "row"),
        P(),
        P(),
        P(),
    )
    return jax.shard_map(
        per_device, mesh=mesh, in_specs=in_specs, out_specs=out_specs, check_vma=False
    )
```

time: 779 us -> 592 us (0.76)
  waiting for transfers between devices: 505 us -> 297 us
  local copies, waits for them, and re-layouts: 29.7 us -> 96.2 us
  blocking collectives: 73.1 us -> 51.5 us
  starting transfers between devices: 12.6 us -> 0.51 us
    reduce_scatter x4 -> x3, waiting for transfers between devices: 261 us -> 12.7 us  [scatter_blocks(): halves = lax.psum_scatter(parts, 'row', scatter_dimension=0, tiled=False)]
    unnamed x11 -> x16, waiting for transfers between devices: 1.85 us -> 126 us
    psum x1, waiting for transfers between devices: 88.1 us -> 27.8 us  [scatter_blocks(): return lax.psum(own, 'dp')]
    reshape x4 -> x12, local copies, waits for them, and re-layouts: 8.81 us -> 50.3 us  [split_blocks(): shaped = value.reshape(first, rows // first, second, columns // second)]
    all_gather x6, waiting for transfers between devices: 154 us -> 131 us  [the longest x3 110 us: gather_blocks(): pieces = lax.all_gather(block, 'col', axis=0, tiled=False)]
    psum x2 -> x1, blocking collectives: 59.3 us -> 43.4 us  [per_device(): sums = lax.psum(jnp.concatenate(parts), ('dp', 'row', 'col'))]
    transpose x0 -> x2, local copies, waits for them, and re-layouts: none -> 15.4 us  [the longest x1 9.42 us: per_device(): outer_full = gather_blocks(outer_weight).transpose(1, 2, 0, 3)]
    all_gather x6, starting transfers between devices: 11.9 us -> 0.23 us  [the longest x3 0.12 us: gather_blocks(): pieces = lax.all_gather(block, 'col', axis=0, tiled=False)]
  transfers between devices with their start and end apart: 11 -> 13, of which waited for: 9 -> 10; matrix products, arithmetic and copies ran while one was open for 7% -> 25% of each run, Pallas kernels for 0% -> 0%
where the time goes in v1:
time: 592 us; the launch traced here: 582 us
  waiting for transfers between devices  297 us (50%)
  matrix products  102 us (17%)
  local copies, waits for them, and re-layouts  96.2 us (16%)
  blocking collectives  51.5 us (9%)
  other arithmetic  20.1 us (3%)
  between operations  15.1 us (3%)
    unnamed x16, waiting for transfers between devices  126 us
    all_gather x3, waiting for transfers between devices, gather_blocks(): pieces = lax.all_gather(block, 'col', axis=0, tiled=False)  110 us
    reshape x12, local copies, waits for them, and re-layouts, split_blocks(): shaped = value.reshape(first, rows // first, second, columns // second)  50.3 us
    psum x1, blocking collectives, per_device(): sums = lax.psum(jnp.concatenate(parts), ('dp', 'row', 'col'))  43.4 us
    psum x1, waiting for transfers between devices, scatter_blocks(): return lax.psum(own, 'dp')  27.8 us
    dot_general x6, matrix products, dot_plain(): return jnp.dot(left, right, preferred_element_type=jnp.float32)  27.7 us
    dot_general x6, matrix products, dot_second(): lax.dot_general(left, right, (((1,), (1,)), ((), ())), preferred_element_...  21.5 us
    all_gather x3, waiting for transfers between devices, gather_blocks(): return lax.all_gather(pieces, 'row', axis=0, tiled=False)  20.6 us
  transfers between devices with their start and end apart: 13, of which 10 were waited for; matrix products, arithmetic and copies ran while one was open for 25% of the time, Pallas kernels for 0%

profile of v1, /device:TPU:0, one launch (start us, length us, event | category | flops | bytes accessed | tf_op | source)
XLA Modules:
  0.0 582.2 jit_solution(14754331359870309615)
XLA Ops:
  7.2 2.0 pad_maximum_fusion
  10.8 39.8 %all-gather.15.cloned.1.call-done = bf16[16,192,384]{2,1,0:T(8,128)(2,1)} async-done(((bf16[4,192,384]{2,1,0:T(8,128)(2,1)}), bf16[16,192,384]{2,1,0:T(8,128)(2,1)}) %all-gather.15.cloned.1.call-update) | async-done | bytes 2359312 | tf_op jit(solution)/shard_map/all_gather | solution.py:15
  50.7 39.3 %all-gather.19.cloned.1.call-done = bf16[1536,768]{1,0:T(8,128)(2,1)} async-done(((bf16[384,768]{1,0:T(8,128)(2,1)}), bf16[1536,768]{1,0:T(8,128)(2,1)}) %all-gather.19.cloned.1.call-update) | async-done | bytes 2359312 | tf_op jit(solution)/shard_map/all_gather | solution.py:15
  90.2 8.1 %all-gather.7 = f32[4,1,1152]{2,1,0:T(1,128)S(1)} all-gather(f32[1,1,1152]{2,1,0:T(1,128)S(1)} %reshape.238), channel_id=4, replica_groups=mesh['dp'=4,'row'=2,'col'=4] {'col'}, dimensions={0}, use_global_device_ids=true | all-gather | bytes 23040 | tf_op jit(solution)/shard_map/all_gather | solution.py:93
  98.3 31.0 %all-gather.23.cloned.1.call-done = bf16[3072,384]{1,0:T(8,128)(2,1)} async-done(((bf16[768,384]{1,0:T(8,128)(2,1)}), bf16[3072,384]{1,0:T(8,128)(2,1)}) %all-gather.23.cloned.1.call-update) | async-done | bytes 2359312 | tf_op jit(solution)/shard_map/all_gather | solution.py:15
  130.9 14.3 %all-gather.17.cloned.1.call-done = bf16[8,4,192,384]{3,2,1,0:T(8,128)(2,1)} async-done(((bf16[4,4,192,384]{3,2,1,0:T(8,128)(2,1)}), bf16[8,4,192,384]{3,2,1,0:T(8,128)(2,1)}) %all-gather.17.cloned.1.call-update) | async-done | bytes 4718608 | tf_op jit(solution)/shard_map/all_gather | solution.py:16
  145.2 2.9 fusion.47
  148.1 1.2 copy.76
  149.6 1.2 copy.77
  150.8 1.2 copy.99
  152.0 1.2 copy.75
  153.5 1.2 copy.79
  154.7 1.2 copy.100
  156.0 6.3 %all-gather.21.cloned.1.call-done = bf16[8,384,768]{2,1,0:T(8,128)(2,1)} async-done(((bf16[4,384,768]{2,1,0:T(8,128)(2,1)}), bf16[8,384,768]{2,1,0:T(8,128)(2,1)}) %all-gather.21.cloned.1.call-update) | async-done | bytes 4718608 | tf_op jit(solution)/shard_map/all_gather | solution.py:16
  162.3 6.0 %copy.80 = bf16[2,384,4,768]{3,2,1,0:T(4,128)(2,1)S(1)} copy(bf16[2,384,4,768]{3,1,2,0:T(8,128)(2,1)} %bitcast.169) | data formatting | bytes 9437184 | tf_op jit(solution)/shard_map/transpose | solution.py:89
  168.3 3.2 copy.101
  172.5 1.7 add_convert_fusion.2
  174.2 1.7 add_convert_fusion.3
  175.9 7.4 %fusion.50 = (f32[12,512]{1,0:T(8,128)S(1)}, f32[12,512,512]{1,2,0:T(8,128)}) fusion(pred[512]{0:T(512)(128)(4,1)S(1)} %iota_compare_fusion, bf16[512,12,64]{0,2,1:T(8,128)(2,1)S(1)} %bitcast.204, bf16[512,12,64]{0,2,1:T(8,128)(2,1)S(1)} %bitcast.182), kind=kOutput, calls=%fused_computation.118 | convolution fusion | flops 415236608 | bytes 14180864 | tf_op jit(solution)/shard_map/sub | solution.py:121
  183.4 6.2 %fusion.22 = bf16[12,64,512]{2,1,0:T(8,128)(2,1)S(1)} fusion(bf16[512,12,64]{0,2,1:T(8,128)(2,1)} %bitcast.215, f32[12,512,512]{1,2,0:T(8,128)} %get-tuple-element.54, f32[12,512]{1,0:T(8,128)S(1)} %get-tuple-element.53), kind=kOutput, calls=%fused_computation.72 | convolution fusion | flops 409337856 | bytes 14180352 | tf_op jit(solution)/shard_map/shqk,skhd->sqhd/dot_general | solution.py:125
  190.9 9.4 %copy.81 = bf16[4,768,2,384]{3,2,1,0:T(2,128)(2,1)} copy(bf16[4,768,2,384]{3,1,0,2:T(8,128)(2,1)} %bitcast.170) | data formatting | bytes 9437184 | tf_op jit(solution)/shard_map/transpose | solution.py:91
  200.3 3.3 copy.102
  203.9 18.6 %multiply_convert_fusion.1 = (bf16[512,3072]{1,0:T(8,128)(2,1)S(1)}, f32[512,3072]{1,0:T(8,128)}, f32[512,3072]{1,0:T(8,128)}) fusion(f32[3072]{0:T(1024)S(1)} %add.141, bf16[768,3072]{1,0:T(8,128)(2,1)S(1)} %bitcast.168, f32[512,768]{1,0:T(8,128)S(1)} %get-tuple-element.56, f32[768]{0:T(1024)S(1)} %copy-done.46, f32[768]{0:T(1024)S(1)} %copy-done.32, ...), kind=kOutput, calls=%fused_computation.10 | convolution fusion | flops 2521694208 | bytes 22042624 | tf_op jit(solution)/shard_map/dot_general | solution.py:32
  222.6 2.8 fusion.52
  226.6 2.1 fusion.43
  228.7 4.4 convolution_convert_fusion
  233.1 10.1 %reshape.230 = bf16[4,768,2,384]{3,2,1,0:T(2,128)(2,1)} reshape(bf16[3072,768]{1,0:T(8,128)(2,1)} %convolution_convert_fusion) | data formatting | bytes 9437184 | tf_op jit(solution)/shard_map/reshape | solution.py:27
  243.2 5.2 copy.110
  248.5 9.3 %convert_reduce_fusion = (f32[3072]{0:T(1024)}, bf16[512,3072]{1,0:T(8,128)(2,1)S(1)}) fusion(f32[512,3072]{1,0:T(8,128)} %get-tuple-element.33, bf16[3072,768]{1,0:T(8,128)(2,1)} %bitcast.173, f32[512,768]{1,0:T(8,128)S(1)} %get-tuple-element.29, f32[512,3072]{1,0:T(8,128)} %get-tuple-element.57, f32[3072]{0:T(1024)S(1)} %add.141), kind=kOutput, calls=%fused_computation.8 | convolution fusion | flops 2443047936 | bytes 22044672 | tf_op jit(solution)/shard_map/dot_general | solution.py:42
  257.7 2.0 copy-done.48
  259.7 4.8 convolution_convert_fusion.1
  264.5 9.7 %reshape.229 = bf16[2,384,4,768]{3,2,1,0:T(4,128)(2,1)} reshape(bf16[768,3072]{1,0:T(8,128)(2,1)} %convolution_convert_fusion.1) | data formatting | bytes 9437184 | tf_op jit(solution)/shard_map/reshape | solution.py:27
  274.3 5.1 copy.111
  279.4 7.0 %multiply_reduce_fusion.1 = (f32[768]{0:T(1024)}, f32[512]{0:T(512)S(1)}, f32[512]{0:T(512)S(1)}, f32[768]{0:T(1024)}, f32[512,768]{1,0:T(8,128)S(1)}) fusion(f32[512,768]{1,0:T(8,128)S(1)} %get-tuple-element.56, f32[512]{0:T(512)S(1)} %add_rsqrt_fusion.1, f32[512]{0:T(512)S(1)} %broadcast_multiply_fusion.5, f32[768]{0:T(1024)S(1)} %copy-done.32, ...), kind=kOutput, calls=%fused_computation.49 | convolution fusion | flops 2419848704 | bytes 12600320 | tf_op jit(solution)/shard_map/dot_general | solution.py:42
  286.3 1.1 fusion.45
  288.6 1.2 copy.82
  290.5 1.4 reshape.228
  291.9 1.5 copy.112
  293.4 7.4 %convert_reduce_fusion.2 = (f32[12,64]{1,0:T(8,128)}, bf16[12,64,512]{2,1,0:T(8,128)(2,1)S(1)}) fusion(bf16[512,12,64]{0,2,1:T(8,128)(2,1)S(1)} %bitcast.198, f32[12,512,512]{1,2,0:T(8,128)} %get-tuple-element.54, f32[12,512]{1,0:T(8,128)S(1)} %copy-done.25), kind=kOutput, calls=%fused_computation.47 | convolution fusion | flops 410123520 | bytes 14183424 | tf_op jit(solution)/shard_map/shqk,sqhd->skhd/dot_general | solution.py:173
  301.7 1.8 convolution_convert_fusion.3
  303.4 3.6 reshape.227
  307.0 2.6 copy.113
  309.6 10.4 %multiply_reduce_fusion = (f32[12,512]{1,0:T(8,128)S(1)}, f32[12,512,512]{1,2,0:T(8,128)}) fusion(f32[12,512,512]{1,2,0:T(8,128)} %get-tuple-element.54, f32[12,512]{1,0:T(8,128)} %copy-done.24, bf16[512,12,64]{0,2,1:T(8,128)(2,1)S(1)} %bitcast.199, bf16[512,12,64]{0,2,1:T(8,128)(2,1)} %bitcast.216), kind=kOutput, calls=%fused_computation.2 | convolution fusion | flops 412084224 | bytes 26787840 | tf_op jit(solution)/shard_map/sqhd,skhd->shqk/dot_general | solution.py:160
  320.0 1.3 slice-done.2
  321.3 6.9 %multiply_convert_fusion = bf16[12,512,512]{1,2,0:T(8,128)(2,1)S(1)} fusion(f32[12,512,512]{1,2,0:T(8,128)} %get-tuple-element.62, f32[12,512]{1,0:T(8,128)S(1)} %get-tuple-element.61, f32[12,512,512]{1,2,0:T(8,128)S(1)} %bitcast.160, f32[12,512]{1,0:T(8,128)S(1)} %copy-done.26), kind=kLoop, calls=%fused_computation.1 | loop fusion | flops 12582912 | bytes 31506432 | tf_op jit(solution)/shard_map/convert_element_type | solution.py:164
  328.2 2.0 multiply_convert_fusion.2
  331.7 1.8 convolution_convert_fusion.4
  333.5 3.6 reshape.226
  337.1 2.5 copy.114
  339.6 4.0 convert_reduce_fusion.3
  343.6 1.8 convolution_convert_fusion.5
  345.4 3.6 reshape.225
  349.0 1.6 copy.115
  351.0 2.5 maximum_bitcast_fusion
  354.9 12.6 %reduce-scatter.13.cloned.1.call-done = bf16[1,4,4,192,384]{4,3,2,1,0:T(8,128)(2,1)} async-done(((bf16[2,4,4,192,384]{4,3,2,1,0:T(8,128)(2,1)}), bf16[1,4,4,192,384]{4,3,2,1,0:T(8,128)(2,1)}) %reduce-scatter.13.cloned.1.call-update) | async-done | bytes 2359312 | tf_op jit(solution)/shard_map/reduce_scatter | solution.py:20
  367.7 41.6 %reduce-scatter.23.cloned.1.call-done = bf16[1,768,384]{2,1,0:T(8,128)(2,1)} async-done(((bf16[4,768,384]{2,1,0:T(8,128)(2,1)}), bf16[1,768,384]{2,1,0:T(8,128)(2,1)}) %reduce-scatter.23.cloned.1.call-update) | async-done | bytes 589840
  409.3 40.8 %reduce-scatter.21.cloned.1.call-done = bf16[1,384,768]{2,1,0:T(8,128)(2,1)} async-done(((bf16[4,384,768]{2,1,0:T(8,128)(2,1)}), bf16[1,384,768]{2,1,0:T(8,128)(2,1)}) %reduce-scatter.21.cloned.1.call-update) | async-done | bytes 589840
  450.1 40.6 %reduce-scatter.19.cloned.1.call-done = bf16[1,4,192,384]{3,2,1,0:T(8,128)(2,1)} async-done(((bf16[4,4,192,384]{3,2,1,0:T(8,128)(2,1)}), bf16[1,4,192,384]{3,2,1,0:T(8,128)(2,1)}) %reduce-scatter.19.cloned.1.call-update) | async-done | bytes 589840
  490.9 43.4 %psum.29 = f32[9216]{0:T(1024)S(1)} all-reduce(f32[9216]{0:T(1024)S(1)} %constant_dynamic-update-slice_fusion), channel_id=1, replica_groups=mesh['dp'=4,'row'=2,'col'=4] {'dp','row','col'}, use_global_device_ids=true, to_apply=%region_23.24 | all-reduce | flops 9216 | bytes 73728 | tf_op jit(solution)/shard_map/psum | solution.py:208
  536.8 2.5 fusion.54
  540.9 2.1 add_add_fusion
  542.9 27.8 %all-reduce.6.cloned.1.call-done = (bf16[4,192,384]{2,1,0:T(8,128)(2,1)}, bf16[384,768]{1,0:T(8,128)(2,1)}, bf16[768,384]{1,0:T(8,128)(2,1)}) async-done(((bf16[4,192,384]{2,1,0:T(8,128)(2,1)}, bf16[384,768]{1,0:T(8,128)(2,1)}, bf16[768,384]{1,0:T(8,128)(2,1)}), (bf16[4,192,384]{2,1,0:T(8,128)(2,1)}, bf16[384,768]{1,0:T(8,128)(2,1)}, bf16[768,384]{1,0:T(8,128)(2,1)})) %all-reduce.6.cloned.1.call-update) | async-done | bytes 1769488 | tf_op jit(solution)/shard_map/psum | solution.py:22
  570.8 1.2 convert_element_type.160
  573.0 1.1 convert_element_type.165
  (183 shorter events, 20.2 us)
Async XLA Ops:
  7.2 43.5 %all-gather.15.cloned.1.call-start = ((), (), s32[]{:S(2)}) async-start(), calls=%async_computation.9 | async-start | bytes 2949120 | tf_op jit(solution)/shard_map/all_gather | solution.py:15
  9.3 80.7 %all-gather.19.cloned.1.call-start = ((), (), s32[]{:S(2)}) async-start(), calls=%async_computation.11 | async-start | bytes 2949120 | tf_op jit(solution)/shard_map/all_gather | solution.py:15
  10.0 119.3 %all-gather.23.cloned.1.call-start = ((), (), s32[]{:S(2)}) async-start(), calls=%async_computation.13 | async-start | bytes 2949120 | tf_op jit(solution)/shard_map/all_gather | solution.py:15
  10.8 134.4 %all-gather.17.cloned.1.call-start = ((), (), s32[]{:S(2)}) async-start(), calls=%async_computation.10 | async-start | bytes 7077888 | tf_op jit(solution)/shard_map/all_gather | solution.py:16
  50.6 39.4 %copy-start.33 = (f32[768]{0:T(1024)S(1)}, f32[768]{0:T(1024)}, u32[]{:S(2)}) copy-start(f32[768]{0:T(1024)} %param.30) | copy-start | bytes 9220
  50.7 39.4 %copy-start.37 = (f32[192]{0:T(256)S(1)}, f32[192]{0:T(256)}, u32[]{:S(2)}) copy-start(f32[192]{0:T(256)} %param.23) | copy-start | bytes 2308
  50.7 39.4 %copy-start.38 = (f32[192]{0:T(256)S(1)}, f32[192]{0:T(256)}, u32[]{:S(2)}) copy-start(f32[192]{0:T(256)} %param.24) | copy-start | bytes 2308
  50.7 111.6 %all-gather.21.cloned.1.call-start = ((), (), s32[]{:S(2)}) async-start(), calls=%async_computation.12 | async-start | bytes 7077888 | tf_op jit(solution)/shard_map/all_gather | solution.py:16
  90.0 39.7 %copy-start.47 = (s32[4]{0:T(128)S(1)}, s32[4]{0:T(128)}, u32[]{:S(2)}) copy-start(s32[4]{0:T(128)} %param.19) | copy-start | bytes 52
  90.0 100.8 %all-gather.25.cloned.1.call-start = ((), (), s32[]{:S(2)}) async-start(), calls=%async_computation.14 | async-start | bytes 7077888 | tf_op jit(solution)/shard_map/all_gather | solution.py:16
  129.4 224.2 %reduce-scatter.17.cloned.1.call-start = ((), (), s32[]{:S(2)}) async-start(), calls=%async_computation.8 | async-start | bytes 7077888 | tf_op jit(solution)/shard_map/reduce_scatter | solution.py:20
  149.6 22.9 %copy-start.9 = (bf16[96,8,2,384]{3,1,2,0:T(8,128)(2,1)}, bf16[96,8,2,384]{3,1,2,0:T(8,128)(2,1)S(1)}, u32[]{:S(2)}) copy-start(bf16[96,8,2,384]{3,1,2,0:T(8,128)(2,1)S(1)} %copy.98) | copy-start | bytes 3538948
  153.5 20.7 %copy-start.4 = (bf16[96,8,2,384]{3,1,2,0:T(8,128)(2,1)}, bf16[96,8,2,384]{3,1,2,0:T(8,128)(2,1)S(1)}, u32[]{:S(2)}) copy-start(bf16[96,8,2,384]{3,1,2,0:T(8,128)(2,1)S(1)} %copy.97) | copy-start | bytes 3538948
  168.2 3.2 copy-start.11
  168.2 3.2 copy-start.39
  172.5 3.4 copy-start.7
  174.2 1.7 copy-start.20
  183.3 6.2 %copy-start.24 = (f32[12,512]{1,0:T(8,128)}, f32[12,512]{1,0:T(8,128)S(1)}, u32[]{:S(2)}) copy-start(f32[12,512]{1,0:T(8,128)S(1)} %get-tuple-element.53) | copy-start | bytes 73732
  183.3 6.2 %copy-start.12 = (bf16[96,8,2,384]{3,1,2,0:T(8,128)(2,1)S(1)}, bf16[96,8,2,384]{3,1,2,0:T(8,128)(2,1)}, u32[]{:S(2)}) copy-start(bf16[96,8,2,384]{3,1,2,0:T(8,128)(2,1)} %copy.100) | copy-start | bytes 3538948
  183.3 6.2 %copy-start.40 = (bf16[512,768]{1,0:T(8,128)(2,1)S(1)}, bf16[512,768]{1,0:T(8,128)(2,1)}, u32[]{:S(2)}) copy-start(bf16[512,768]{1,0:T(8,128)(2,1)} %param.18) | copy-start | bytes 2359300
  183.4 6.2 %copy-start.44 = (f32[768]{0:T(1024)S(1)}, f32[768]{0:T(1024)}, u32[]{:S(2)}) copy-start(f32[768]{0:T(1024)} %param.26) | copy-start | bytes 9220
  190.9 12.7 %slice-start.3 = ((s8[4718592]{0:T(1024)(128)(4,1)}), s8[524288]{0:T(1024)(128)(4,1)S(1)}, s32[]{:S(2)}) async-start(s8[4718592]{0:T(1024)(128)(4,1)} %bitcast.166), calls=%async_computation.22 | async-start | bytes 1048576
  200.3 3.6 slice-start.4
  200.3 3.6 copy-start.32
  200.3 3.6 copy-start.46
  203.6 19.0 %copy-start.3 = (bf16[384,8,2,384]{3,1,2,0:T(8,128)(2,1)}, bf16[384,8,2,384]{3,1,2,0:T(8,128)(2,1)S(1)}, u32[]{:S(2)}) copy-start(bf16[384,8,2,384]{3,1,2,0:T(8,128)(2,1)S(1)} %copy.102) | copy-start | bytes 14155780
  203.9 18.7 %copy-start.45 = (f32[768]{0:T(1024)S(1)}, f32[768]{0:T(1024)}, u32[]{:S(2)}) copy-start(f32[768]{0:T(1024)} %param.32) | copy-start | bytes 9220
  222.6 3.2 copy-start.6
  222.6 3.2 copy-start.28
  225.4 1.2 copy-start.36
  248.4 105.8 %reduce-scatter.15.cloned.1.call-start = ((), (), s32[]{:S(2)}) async-start(), calls=%async_computation.7 | async-start | bytes 7077888 | tf_op jit(solution)/shard_map/reduce_scatter | solution.py:20
  257.7 2.0 copy-start.48
  279.3 88.2 %reduce-scatter.13.cloned.1.call-start = ((), (), s32[]{:S(2)}) async-start(), calls=%async_computation.6 | async-start | bytes 7077888 | tf_op jit(solution)/shard_map/reduce_scatter | solution.py:20
  286.3 1.4 copy-start.13
  287.7 2.0 copy-start.15
  290.5 2.9 copy-start.16
  291.9 1.5 copy-start.25
  293.4 8.3 %copy-start.41 = (bf16[512,768]{1,0:T(8,128)(2,1)S(1)}, bf16[512,768]{1,0:T(8,128)(2,1)}, u32[]{:S(2)}) copy-start(bf16[512,768]{1,0:T(8,128)(2,1)} %param.18) | copy-start | bytes 2359300
  307.0 13.0 %slice-start = ((s8[12582912]{0:T(1024)(128)(4,1)}), s8[4194304]{0:T(1024)(128)(4,1)S(1)}, s32[]{:S(2)}) async-start(s8[12582912]{0:T(1024)(128)(4,1)} %bitcast.159), calls=%async_computation.19 | async-start | bytes 8388608
  309.6 10.4 %slice-start.1 = ((s8[12582912]{0:T(1024)(128)(4,1)}), s8[4194304]{0:T(1024)(128)(4,1)S(1)}, s32[]{:S(2)}) async-start(s8[12582912]{0:T(1024)(128)(4,1)} %bitcast.159), calls=%async_computation.20 | async-start | bytes 8388608
  309.6 11.7 %slice-start.2 = ((s8[12582912]{0:T(1024)(128)(4,1)}), s8[4194304]{0:T(1024)(128)(4,1)S(1)}, s32[]{:S(2)}) async-start(s8[12582912]{0:T(1024)(128)(4,1)} %bitcast.159), calls=%async_computation.21 | async-start | bytes 8388608
  309.6 11.7 %copy-start.26 = (f32[12,512]{1,0:T(8,128)S(1)}, f32[12,512]{1,0:T(8,128)}, u32[]{:S(2)}) copy-start(f32[12,512]{1,0:T(8,128)} %copy-done.24) | copy-start | bytes 73732
  321.3 6.9 %copy-start.21 = (bf16[768,512]{1,0:T(8,128)(2,1)S(1)}, bf16[768,512]{1,0:T(8,128)(2,1)}, u32[]{:S(2)}) copy-start(bf16[768,512]{1,0:T(8,128)(2,1)} %add_convert_fusion.2) | copy-start | bytes 2359300
  328.2 2.6 copy-start
  328.2 3.5 copy-start.42
  337.1 2.5 copy-start.8
  339.6 4.0 copy-start.43
  349.0 1.6 copy-start.1
  349.0 2.0 copy-start.2
  353.5 55.8 %reduce-scatter.23.cloned.1.call-start = ((), (), s32[]{:S(2)}) async-start(), calls=%async_computation.17 | async-start | bytes 2949120
  354.1 95.9 %reduce-scatter.21.cloned.1.call-start = ((), (), s32[]{:S(2)}) async-start(), calls=%async_computation.16 | async-start | bytes 2949120
  354.2 13.4 %copy-start.27 = (f32[768]{0:T(1024)S(1)}, f32[768]{0:T(1024)}, u32[]{:S(2)}) copy-start(f32[768]{0:T(1024)} %get-tuple-element.30) | copy-start | bytes 9220
  354.2 13.4 %copy-start.35 = (f32[768]{0:T(1024)S(1)}, f32[768]{0:T(1024)}, u32[]{:S(2)}) copy-start(f32[768]{0:T(1024)} %get-tuple-element.17) | copy-start | bytes 9220
  354.2 13.5 %copy-start.34 = (f32[768]{0:T(1024)S(1)}, f32[768]{0:T(1024)}, u32[]{:S(2)}) copy-start(f32[768]{0:T(1024)} %get-tuple-element.22) | copy-start | bytes 9220
  354.2 13.5 %copy-start.29 = (f32[768]{0:T(1024)S(1)}, f32[768]{0:T(1024)}, u32[]{:S(2)}) copy-start(f32[768]{0:T(1024)} %get-tuple-element.28) | copy-start | bytes 9220
  354.8 135.9 %copy-start.31 = (f32[12,64]{1,0:T(8,128)S(1)}, f32[12,64]{1,0:T(8,128)}, u32[]{:S(2)}) copy-start(f32[12,64]{1,0:T(8,128)} %get-tuple-element.65) | copy-start | bytes 9220
  354.9 136.0 %copy-start.30 = (f32[3072]{0:T(1024)S(1)}, f32[3072]{0:T(1024)}, u32[]{:S(2)}) copy-start(f32[3072]{0:T(1024)} %get-tuple-element.67) | copy-start | bytes 36868
  354.9 135.8 %reduce-scatter.19.cloned.1.call-start = ((), (), s32[]{:S(2)}) async-start(), calls=%async_computation.15 | async-start | bytes 2949120
  367.6 203.2 %all-reduce.6.cloned.1.call-start = ((), (), s32[]{:S(2)}) async-start(), calls=%async_computation.18 | async-start | bytes 3538944 | tf_op jit(solution)/shard_map/psum | solution.py:22
  536.8 2.5 copy-start.10
  539.3 1.3 copy-start.5
  539.3 1.6 copy-start.18
  570.8 2.2 copy-start.23
  572.0 2.1 copy-start.22
  (3 other events, 2.7 us)
Sparse Core Ops, SparseCore 0:
  10.4 40.1 all-gather.14
  52.5 37.4 all-gather.18
  91.8 37.4 all-gather.22
  130.7 14.4 all-gather.16
  146.6 15.6 all-gather.20
  163.6 15.6 all-gather.24
  248.5 13.7 reduce-scatter.16
  279.5 13.7 reduce-scatter.14
  353.6 13.8 reduce-scatter.12
  370.7 38.5 reduce-scatter.22
  412.7 37.3 reduce-scatter.20
  453.3 37.3 reduce-scatter.18
  493.4 77.3 all-reduce.5

commit v2 on v1

--- a/solution.py
+++ b/solution.py
@@ -3,6 +3,8 @@
 import jax
 import jax.numpy as jnp
 from jax import lax
+from jax.experimental import pallas as pl
+from jax.experimental.pallas import tpu as pltpu
 from jax.sharding import PartitionSpec as P
 
 HD = 64
@@ -11,9 +13,120 @@
 EPSILON = 1e-05
 
 
-def gather_blocks(block):
-    pieces = lax.all_gather(block, "col", axis=0, tiled=False)
-    return lax.all_gather(pieces, "row", axis=0, tiled=False)
+MESH = pl.DeviceIdType.MESH
+
+
+def gather_kernel(flips, cols, *refs):
+    count = len(flips)
+    shards, fulls = refs[:count], refs[count : 2 * count]
+    local, send, recv, pair_send, pair_recv = refs[2 * count :]
+    me_row, me_col = lax.axis_index("row"), lax.axis_index("col")
+    partner = 1 - me_row
+
+    def place(which, row, col):
+        rows, columns = shards[which].shape
+        first, second = (row, col) if flips[which] else (col, row)
+        return fulls[which].at[
+            pl.ds(pl.multiple_of(first * rows, rows), rows),
+            pl.ds(pl.multiple_of(second * columns, columns), columns),
+        ]
+
+    def to_col(which, step):
+        return pltpu.make_async_remote_copy(
+            src_ref=shards[which],
+            dst_ref=place(which, me_row, me_col),
+            send_sem=send.at[step - 1, which],
+            recv_sem=recv.at[step - 1, which],
+            device_id={"col": lax.rem(me_col + step, cols)},
+            device_id_type=MESH,
+        )
+
+    def from_col(which, step):
+        source = lax.rem(me_col + cols - step, cols)
+        return pltpu.make_async_remote_copy(
+            src_ref=shards[which],
+            dst_ref=place(which, me_row, source),
+            send_sem=send.at[step - 1, which],
+            recv_sem=recv.at[step - 1, which],
+            device_id={"col": lax.rem(me_col + step, cols)},
+            device_id_type=MESH,
+        )
+
+    def to_pair(which, step):
+        source = lax.rem(me_col + cols - step, cols)
+        here = place(which, me_row, source)
+        return pltpu.make_async_remote_copy(
+            src_ref=shards[which] if step == 0 else here,
+            dst_ref=here,
+            send_sem=pair_send.at[step, which],
+            recv_sem=pair_recv.at[step, which],
+            device_id={"row": partner},
+            device_id_type=MESH,
+        )
+
+    def from_pair(which, step):
+        source = lax.rem(me_col + cols - step, cols)
+        return pltpu.make_async_remote_copy(
+            src_ref=shards[which],
+            dst_ref=place(which, partner, source),
+            send_sem=pair_send.at[step, which],
+            recv_sem=pair_recv.at[step, which],
+            device_id={"row": partner},
+            device_id_type=MESH,
+        )
+
+    barrier = pltpu.get_barrier_semaphore()
+    for step in range(1, cols):
+        pl.semaphore_signal(
+            barrier, inc=1, device_id={"col": lax.rem(me_col + step, cols)}, device_id_type=MESH
+        )
+    pl.semaphore_signal(barrier, inc=1, device_id={"row": partner}, device_id_type=MESH)
+    pl.semaphore_wait(barrier, cols)
+    for which in range(count):
+        for step in range(1, cols):
+            to_col(which, step).start()
+        to_pair(which, 0).start()
+        pltpu.make_async_copy(
+            shards[which], place(which, me_row, me_col), local.at[which]
+        ).start()
+    for which in range(count):
+        for step in range(1, cols):
+            from_col(which, step).wait_recv()
+            to_pair(which, step).start()
+    for which in range(count):
+        pltpu.make_async_copy(
+            shards[which], place(which, me_row, me_col), local.at[which]
+        ).wait()
+        for step in range(cols):
+            from_pair(which, step).wait_recv()
+            to_pair(which, step).wait_send()
+            if step:
+                to_col(which, step).wait_send()
+
+
+def gather_weights(collective, flips, shards):
+    cols, rows = lax.axis_size("col"), lax.axis_size("row")
+    fulls = []
+    for shard, flip in zip(shards, flips):
+        first, second = (rows, cols) if flip else (cols, rows)
+        fulls.append(
+            jax.ShapeDtypeStruct((shard.shape[0] * first, shard.shape[1] * second), shard.dtype)
+        )
+    count = len(shards)
+    return pl.pallas_call(
+        partial(gather_kernel, flips, cols),
+        out_shape=fulls,
+        in_specs=[pl.BlockSpec(memory_space=pl.ANY)] * count,
+        out_specs=[pl.BlockSpec(memory_space=pl.ANY)] * count,
+        scratch_shapes=[
+            pltpu.SemaphoreType.DMA((count,)),
+            pltpu.SemaphoreType.DMA((cols - 1, count)),
+            pltpu.SemaphoreType.DMA((cols - 1, count)),
+            pltpu.SemaphoreType.DMA((cols, count)),
+            pltpu.SemaphoreType.DMA((cols, count)),
+        ],
+        compiler_params=pltpu.CompilerParams(collective_id=collective, has_side_effects=True),
+    )(*shards)
 
 
 def scatter_blocks(parts):
@@ -83,13 +196,11 @@
     f32 = jnp.float32
     row_size, col_size = lax.axis_size("row"), lax.axis_size("col")
     col_rank = lax.axis_index("col")
-    small = gather_blocks(jnp.stack([query_weight, key_weight, value_weight, output_weight]))
-    small = small.transpose(2, 1, 3, 0, 4).reshape(4, small.shape[3] * col_size, -1)
-    query_full, key_full, value_full, output_full = (small[i] for i in range(4))
-    inner_full = gather_blocks(inner_weight).transpose(0, 2, 1, 3)
-    inner_full = inner_full.reshape(hidden_in.shape[1], -1)
-    outer_full = gather_blocks(outer_weight).transpose(1, 2, 0, 3)
-    outer_full = outer_full.reshape(-1, hidden_in.shape[1])
+    query_full, key_full, value_full, output_full, inner_full, outer_full = gather_weights(
+        0,
+        (False, False, False, False, True, False),
+        (query_weight, key_weight, value_weight, output_weight, inner_weight, outer_weight),
+    )
     biases = lax.all_gather(
         jnp.concatenate([query_bias, value_bias, inner_bias]), "col", axis=0, tiled=False
     )

time: 592 us -> 513 us (0.87)
  waiting for transfers between devices: 297 us -> 164 us
  Pallas kernels: 0 us -> 82.6 us
  local copies, waits for them, and re-layouts: 96.2 us -> 66.5 us
    all_gather x6 -> x0, waiting for transfers between devices: 131 us -> none  [the longest x3 110 us: gather_blocks(): pieces = lax.all_gather(block, 'col', axis=0, tiled=False)]
    pallas_call x0 -> x1, Pallas kernels: none -> 82.6 us  [gather_weights(): pl.pallas_call(partial(gather_kernel, flips, cols), out_shape=fulls, in_s...]
    transpose x2 -> x0, local copies, waits for them, and re-layouts: 15.4 us -> none  [the longest x1 9.42 us: per_device(): outer_full = gather_blocks(outer_weight).transpose(1, 2, 0, 3)]
    unnamed x124 -> x110, local copies, waits for them, and re-layouts: 17 us -> 9.02 us
    slice x5 -> x0, local copies, waits for them, and re-layouts: 7.74 us -> none  [per_device(): query_full, key_full, value_full, output_full = (small[i] for i in range(4))]
    unnamed x16 -> x10, waiting for transfers between devices: 126 us -> 124 us
  transfers between devices with their start and end apart: 13 -> 7, of which waited for: 10 -> 5; matrix products, arithmetic and copies ran while one was open for 25% -> 20% of each run, Pallas kernels for 0% -> 0%
where the time goes in v2:
time: 513 us; the launch traced here: 506 us
  waiting for transfers between devices  164 us (32%)
  matrix products  107 us (21%)
  Pallas kernels  82.6 us (16%)
  local copies, waits for them, and re-layouts  66.5 us (13%)
  blocking collectives  52.2 us (10%)
  other arithmetic  18.1 us (4%)
  between operations  15.1 us (3%)
    unnamed x10, waiting for transfers between devices  124 us
    pallas_call x1, Pallas kernels, gather_weights(): pl.pallas_call(partial(gather_kernel, flips, cols), out_shape=fulls, in_s...  82.6 us
    reshape x12, local copies, waits for them, and re-layouts, split_blocks(): shaped = value.reshape(first, rows // first, second, columns // second)  50.4 us
    psum x1, blocking collectives, per_device(): sums = lax.psum(jnp.concatenate(parts), ('dp', 'row', 'col'))  42.6 us
    dot_general x6, matrix products, dot_plain(): return jnp.dot(left, right, preferred_element_type=jnp.float32)  31.3 us
    psum x1, waiting for transfers between devices, scatter_blocks(): return lax.psum(own, 'dp')  29 us
    dot_general x6, matrix products, dot_second(): lax.dot_general(left, right, (((1,), (1,)), ((), ())), preferred_element_...  20.7 us
    dot_general x6, matrix products, dot_first(): lax.dot_general(left, right, (((0,), (0,)), ((), ())), preferred_element_...  17.7 us
  transfers between devices with their start and end apart: 7, of which 5 were waited for; matrix products, arithmetic and copies ran while one was open for 20% of the time, Pallas kernels for 0%

profile of v2, /device:TPU:0, one launch (start us, length us, event | category | flops | bytes accessed | tf_op | source)
XLA Modules:
  0.0 506.0 jit_solution(990002501453379657)
XLA Ops:
  7.2 0.8 concatenate.6
  8.0 9.6 %all-gather.1 = f32[4,1,1152]{2,1,0:T(1,128)S(1)} all-gather(f32[1,1,1152]{2,1,0:T(1,128)S(1)} %reshape.215), channel_id=2, replica_groups=mesh['dp'=4,'row'=2,'col'=4] {'col'}, dimensions={0}, use_global_device_ids=true | all-gather | bytes 23040 | tf_op jit(solution)/shard_map/all_gather | solution.py:204
  17.7 1.2 dynamic_slice.12
  19.0 0.6 iota_compare_fusion
  19.8 82.6 %shard_map.305 = (bf16[768,768]{1,0:T(8,128)(2,1)}, bf16[768,768]{1,0:T(8,128)(2,1)}, bf16[768,768]{1,0:T(8,128)(2,1)}, bf16[768,768]{1,0:T(8,128)(2,1)}, bf16[7...) custom-call(bf16[192,384]{1,0:T(8,128)(2,1)} %refs_0_.1, bf16[192,384]{1,0:T(8,128)(2,1)} %refs_1_.1, ...), custom_call_target="tpu_custom_call" | custom-call | tf_op jit(solution)/shard_map/pallas_call | solution.py:116
  102.4 2.4 convolution_convert_fusion.7
  104.9 0.8 add_convert_fusion.2
  105.7 0.7 copy-done.8
  106.4 0.8 add_convert_fusion.3
  107.2 7.4 %fusion.49 = (f32[12,512]{1,0:T(8,128)S(1)}, f32[12,512,512]{1,2,0:T(8,128)}) fusion(pred[512]{0:T(512)(128)(4,1)S(1)} %iota_compare_fusion, bf16[512,12,64]{0,2,1:T(8,128)(2,1)S(1)} %bitcast.144, bf16[512,12,64]{0,2,1:T(8,128)(2,1)S(1)} %bitcast.131), kind=kOutput, calls=%fused_computation.116 | convolution fusion | flops 415236608 | bytes 14180864 | tf_op jit(solution)/shard_map/sub | solution.py:232
  114.7 5.9 %fusion.22 = bf16[12,64,512]{2,1,0:T(8,128)(2,1)S(1)} fusion(bf16[512,12,64]{0,2,1:T(8,128)(2,1)S(1)} %bitcast.151, f32[12,512,512]{1,2,0:T(8,128)} %get-tuple-element.62, f32[12,512]{1,0:T(8,128)S(1)} %get-tuple-element.61), kind=kOutput, calls=%fused_computation.72 | convolution fusion | flops 409337856 | bytes 14180352 | tf_op jit(solution)/shard_map/shqk,skhd->sqhd/dot_general | solution.py:236
  120.7 0.9 fusion.50
  122.0 19.2 %multiply_convert_fusion.1 = (bf16[512,3072]{1,0:T(8,128)(2,1)S(1)}, f32[512,3072]{1,0:T(8,128)S(1)}, f32[512,3072]{1,0:T(8,128)}) fusion(f32[3072]{0:T(1024)S(1)} %add.141, bf16[768,3072]{1,0:T(8,128)(2,1)} %get-tuple-element.27, f32[512,768]{1,0:T(8,128)S(1)} %get-tuple-element.64, f32[768]{0:T(1024)S(1)} %copy-done.43, f32[768]{0:T(1024)S(1)} %copy-done.28, ...), kind=kOutput, calls=%fused_computation.10 | convolution fusion | flops 2521694208 | bytes 22042624 | tf_op jit(solution)/shard_map/dot_general | solution.py:145
  141.3 6.2 %fusion.51 = (f32[512]{0:T(512)S(1)}, f32[512,768]{1,0:T(8,128)S(1)}) fusion(f32[768]{0:T(1024)S(1)} %copy-done.43, f32[768]{0:T(1024)S(1)} %copy-done.28, f32[512]{0:T(512)S(1)} %add_rsqrt_fusion.1, f32[512,768]{1,0:T(8,128)S(1)} %get-tuple-element.64, f32[512]{0:T(512)S(1)} %broadcast_multiply_fusion.5, f32[768]{0:T(1024)S(1)} %copy-done.42, ...), kind=kOutput, calls=%fused_computation.118 | convolution fusion | flops 2418671104 | bytes 11025408 | tf_op jit(solution)/shard_map/dot_general | solution.py:145
  147.9 0.8 fusion.21
  148.7 2.1 fusion.43
  150.8 8.9 %convert_reduce_fusion = (f32[3072]{0:T(1024)}, bf16[512,3072]{1,0:T(8,128)(2,1)S(1)}) fusion(f32[512,3072]{1,0:T(8,128)S(1)} %get-tuple-element.45, bf16[3072,768]{1,0:T(8,128)(2,1)} %get-tuple-element.28, f32[512,768]{1,0:T(8,128)S(1)} %get-tuple-element.41, f32[512,3072]{1,0:T(8,128)} %get-tuple-element.65, f32[3072]{0:T(1024)S(1)} %add.141), kind=kOutput, calls=%fused_computation.8 | convolution fusion | flops 2443047936 | bytes 22044672 | tf_op jit(solution)/shard_map/dot_general | solution.py:155
  159.7 1.7 copy-done.46
  161.4 4.9 convolution_convert_fusion.1
  166.2 9.8 %reshape.212 = bf16[2,384,4,768]{3,2,1,0:T(4,128)(2,1)} reshape(bf16[768,3072]{1,0:T(8,128)(2,1)} %convolution_convert_fusion.1) | data formatting | bytes 9437184 | tf_op jit(solution)/shard_map/reshape | solution.py:140
  176.0 5.1 %copy.82 = bf16[2,384,4,768]{3,1,2,0:T(8,128)(2,1)} copy(bf16[2,384,4,768]{3,2,1,0:T(4,128)(2,1)} %reshape.212) | data formatting | bytes 9437184 | tf_op jit(solution)/shard_map/reshape | solution.py:140
  181.2 1.3 copy-done.7
  182.5 6.6 %convolution_convert_fusion = bf16[3072,768]{1,0:T(8,128)(2,1)} fusion(bf16[512,3072]{1,0:T(8,128)(2,1)} %copy-done.45, f32[512,768]{1,0:T(8,128)S(1)} %copy-done.7), kind=kOutput, calls=%fused_computation.28 | convolution fusion | flops 2418671616 | bytes 9437184 | tf_op jit(solution)/shard_map/dot_general | solution.py:149
  189.2 10.3 %reshape.213 = bf16[4,768,2,384]{3,2,1,0:T(2,128)(2,1)} reshape(bf16[3072,768]{1,0:T(8,128)(2,1)} %convolution_convert_fusion) | data formatting | bytes 9437184 | tf_op jit(solution)/shard_map/reshape | solution.py:140
  199.5 5.1 copy.81
  204.6 7.0 %multiply_reduce_fusion.1 = (f32[768]{0:T(1024)}, f32[512]{0:T(512)S(1)}, f32[512]{0:T(512)S(1)}, f32[768]{0:T(1024)}, f32[512,768]{1,0:T(8,128)S(1)}) fusion(f32[512,768]{1,0:T(8,128)S(1)} %get-tuple-element.64, f32[512]{0:T(512)S(1)} %add_rsqrt_fusion.1, f32[512]{0:T(512)S(1)} %broadcast_multiply_fusion.5, f32[768]{0:T(1024)S(1)} %copy-done.28, ...), kind=kOutput, calls=%fused_computation.49 | convolution fusion | flops 2419848704 | bytes 12600320 | tf_op jit(solution)/shard_map/dot_general | solution.py:155
  211.6 1.1 fusion.45
  212.9 0.8 convolution_convert_fusion.6
  213.7 1.2 copy.59
  214.9 0.8 convolution_convert_fusion.2
  215.7 1.3 reshape.211
  217.0 1.4 copy.83
  218.5 7.4 %convert_reduce_fusion.2 = (f32[12,64]{1,0:T(8,128)}, bf16[12,64,512]{2,1,0:T(8,128)(2,1)S(1)}) fusion(bf16[512,12,64]{0,2,1:T(8,128)(2,1)S(1)} %bitcast.138, f32[12,512,512]{1,2,0:T(8,128)} %get-tuple-element.62, f32[12,512]{1,0:T(8,128)} %copy-done.21), kind=kOutput, calls=%fused_computation.47 | convolution fusion | flops 410123520 | bytes 14183424 | tf_op jit(solution)/shard_map/shqk,sqhd->skhd/dot_general | solution.py:284
  225.9 0.9 copy-done.13
  226.8 1.8 convolution_convert_fusion.3
  228.6 3.6 reshape.210
  232.1 2.6 copy.84
  234.7 10.4 %multiply_reduce_fusion = (f32[12,512]{1,0:T(8,128)S(1)}, f32[12,512,512]{1,2,0:T(8,128)}) fusion(f32[12,512,512]{1,2,0:T(8,128)} %get-tuple-element.62, f32[12,512]{1,0:T(8,128)} %copy-done.21, bf16[512,12,64]{0,2,1:T(8,128)(2,1)S(1)} %bitcast.139, bf16[512,12,64]{0,2,1:T(8,128)(2,1)} %bitcast.152), kind=kOutput, calls=%fused_computation.2 | convolution fusion | flops 412084224 | bytes 26787840 | tf_op jit(solution)/shard_map/sqhd,skhd->shqk/dot_general | solution.py:271
  245.1 1.3 slice-done.2
  246.4 6.9 %multiply_convert_fusion = bf16[12,512,512]{1,2,0:T(8,128)(2,1)S(1)} fusion(f32[12,512,512]{1,2,0:T(8,128)} %get-tuple-element.70, f32[12,512]{1,0:T(8,128)S(1)} %get-tuple-element.69, f32[12,512,512]{1,2,0:T(8,128)S(1)} %bitcast.124, f32[12,512]{1,0:T(8,128)S(1)} %copy-done.22), kind=kLoop, calls=%fused_computation.1 | loop fusion | flops 12582912 | bytes 31506432 | tf_op jit(solution)/shard_map/convert_element_type | solution.py:275
  253.3 2.0 multiply_convert_fusion.2
  256.0 0.9 copy-done.15
  256.9 1.8 convolution_convert_fusion.4
  258.6 3.6 reshape.209
  262.2 2.5 copy.85
  264.7 4.0 convert_reduce_fusion.3
  268.8 1.8 convolution_convert_fusion.5
  270.6 3.6 reshape.208
  274.1 1.6 copy.86
  276.1 2.5 maximum_bitcast_fusion
  279.8 11.5 %reduce-scatter.13.cloned.1.call-done = bf16[1,4,4,192,384]{4,3,2,1,0:T(8,128)(2,1)} async-done(((bf16[2,4,4,192,384]{4,3,2,1,0:T(8,128)(2,1)}), bf16[1,4,4,192,384]{4,3,2,1,0:T(8,128)(2,1)}) %reduce-scatter.13.cloned.1.call-update) | async-done | bytes 2359312 | tf_op jit(solution)/shard_map/reduce_scatter | solution.py:133
  291.5 41.6 %reduce-scatter.21.cloned.1.call-done = bf16[1,384,768]{2,1,0:T(8,128)(2,1)} async-done(((bf16[4,384,768]{2,1,0:T(8,128)(2,1)}), bf16[1,384,768]{2,1,0:T(8,128)(2,1)}) %reduce-scatter.21.cloned.1.call-update) | async-done | bytes 589840
  333.1 40.6 %reduce-scatter.23.cloned.1.call-done = bf16[1,768,384]{2,1,0:T(8,128)(2,1)} async-done(((bf16[4,768,384]{2,1,0:T(8,128)(2,1)}), bf16[1,768,384]{2,1,0:T(8,128)(2,1)}) %reduce-scatter.23.cloned.1.call-update) | async-done | bytes 589840
  373.7 40.6 %reduce-scatter.19.cloned.1.call-done = bf16[1,4,192,384]{3,2,1,0:T(8,128)(2,1)} async-done(((bf16[4,4,192,384]{3,2,1,0:T(8,128)(2,1)}), bf16[1,4,192,384]{3,2,1,0:T(8,128)(2,1)}) %reduce-scatter.19.cloned.1.call-update) | async-done | bytes 589840
  414.5 42.6 %psum.29 = f32[9216]{0:T(1024)S(1)} all-reduce(f32[9216]{0:T(1024)S(1)} %constant_dynamic-update-slice_fusion), channel_id=1, replica_groups=mesh['dp'=4,'row'=2,'col'=4] {'dp','row','col'}, use_global_device_ids=true, to_apply=%region_23.24 | all-reduce | flops 9216 | bytes 73728 | tf_op jit(solution)/shard_map/psum | solution.py:319
  459.0 0.7 dynamic_slice.15
  459.7 2.1 fusion.53
  461.8 0.8 fusion.52
  463.4 2.1 add_add_fusion
  465.4 29.0 %all-reduce.6.cloned.1.call-done = (bf16[4,192,384]{2,1,0:T(8,128)(2,1)}, bf16[384,768]{1,0:T(8,128)(2,1)}, bf16[768,384]{1,0:T(8,128)(2,1)}) async-done(((bf16[4,192,384]{2,1,0:T(8,128)(2,1)}, bf16[384,768]{1,0:T(8,128)(2,1)}, bf16[768,384]{1,0:T(8,128)(2,1)}), (bf16[4,192,384]{2,1,0:T(8,128)(2,1)}, bf16[384,768]{1,0:T(8,128)(2,1)}, bf16[768,384]{1,0:T(8,128)(2,1)})) %all-reduce.6.cloned.1.call-update) | async-done | bytes 1769488 | tf_op jit(solution)/shard_map/psum | solution.py:135
  494.5 1.2 convert_element_type.160
  495.7 1.0 slice_bitcast_fusion
  496.7 1.1 convert_element_type.165
  497.8 1.1 convert_element_type.167
  (143 shorter events, 6.5 us)
Async XLA Ops:
  7.2 271.5 %reduce-scatter.15.cloned.1.call-start = ((), (), s32[]{:S(2)}) async-start(), calls=%async_computation.7 | async-start | bytes 7077888 | tf_op jit(solution)/shard_map/reduce_scatter | solution.py:133
  102.4 2.5 copy-start.32
  102.4 2.5 copy-start.36
  104.8 2.4 copy-start.4
  104.9 1.6 copy-start.8
  105.7 9.0 %copy-start.17 = (bf16[768,512]{1,0:T(8,128)(2,1)}, bf16[768,512]{1,0:T(8,128)(2,1)S(1)}, u32[]{:S(2)}) copy-start(bf16[768,512]{1,0:T(8,128)(2,1)S(1)} %add_convert_fusion.2) | copy-start | bytes 2359300
  107.2 7.5 %copy-start.44 = (bf16[768,512]{1,0:T(8,128)(2,1)}, bf16[768,512]{1,0:T(8,128)(2,1)S(1)}, u32[]{:S(2)}) copy-start(bf16[768,512]{1,0:T(8,128)(2,1)S(1)} %add_convert_fusion.3) | copy-start | bytes 2359300
  114.7 6.0 %copy-start.21 = (f32[12,512]{1,0:T(8,128)}, f32[12,512]{1,0:T(8,128)S(1)}, u32[]{:S(2)}) copy-start(f32[12,512]{1,0:T(8,128)S(1)} %get-tuple-element.61) | copy-start | bytes 73732
  114.7 6.0 %copy-start.34 = (bf16[768,768]{1,0:T(8,128)(2,1)S(1)}, bf16[768,768]{1,0:T(8,128)(2,1)}, u32[]{:S(2)}) copy-start(bf16[768,768]{1,0:T(8,128)(2,1)} %get-tuple-element.26) | copy-start | bytes 3538948
  114.7 6.0 %copy-start.37 = (bf16[512,768]{1,0:T(8,128)(2,1)S(1)}, bf16[512,768]{1,0:T(8,128)(2,1)}, u32[]{:S(2)}) copy-start(bf16[512,768]{1,0:T(8,128)(2,1)} %param.18) | copy-start | bytes 2359300
  114.7 6.0 %copy-start.41 = (f32[768]{0:T(1024)S(1)}, f32[768]{0:T(1024)}, u32[]{:S(2)}) copy-start(f32[768]{0:T(1024)} %param.26) | copy-start | bytes 9220
  120.7 1.3 copy-start.10
  120.7 1.3 copy-start.28
  120.7 1.3 copy-start.43
  122.0 19.2 %copy-start.42 = (f32[768]{0:T(1024)S(1)}, f32[768]{0:T(1024)}, u32[]{:S(2)}) copy-start(f32[768]{0:T(1024)} %param.32) | copy-start | bytes 9220
  141.2 6.3 %copy-start.45 = (bf16[512,3072]{1,0:T(8,128)(2,1)}, bf16[512,3072]{1,0:T(8,128)(2,1)S(1)}, u32[]{:S(2)}) copy-start(bf16[512,3072]{1,0:T(8,128)(2,1)S(1)} %get-tuple-element.44) | copy-start | bytes 9437188
  141.2 6.6 %copy-start.3 = (bf16[512,768]{1,0:T(8,128)(2,1)S(1)}, bf16[512,768]{1,0:T(8,128)(2,1)}, u32[]{:S(2)}) copy-start(bf16[512,768]{1,0:T(8,128)(2,1)} %param.35) | copy-start | bytes 2359300
  141.2 6.6 %copy-start.24 = (f32[768]{0:T(1024)S(1)}, f32[768]{0:T(1024)}, u32[]{:S(2)}) copy-start(f32[768]{0:T(1024)} %param.33) | copy-start | bytes 9220
  147.5 1.1 copy-start.31
  150.8 8.9 %copy-start.6 = (f32[512,768]{1,0:T(8,128)}, f32[512,768]{1,0:T(8,128)S(1)}, u32[]{:S(2)}) copy-start(f32[512,768]{1,0:T(8,128)S(1)} %get-tuple-element.41) | copy-start | bytes 4718596
  159.7 1.7 copy-start.46
  181.1 1.4 copy-start.7
  181.1 98.1 %reduce-scatter.17.cloned.1.call-start = ((), (), s32[]{:S(2)}) async-start(), calls=%async_computation.8 | async-start | bytes 7077888 | tf_op jit(solution)/shard_map/reduce_scatter | solution.py:133
  204.6 86.8 %reduce-scatter.13.cloned.1.call-start = ((), (), s32[]{:S(2)}) async-start(), calls=%async_computation.6 | async-start | bytes 7077888 | tf_op jit(solution)/shard_map/reduce_scatter | solution.py:133
  211.6 1.3 copy-start.35
  212.7 2.2 copy-start.11
  215.7 2.8 copy-start.12
  218.5 8.3 %copy-start.38 = (bf16[512,768]{1,0:T(8,128)(2,1)S(1)}, bf16[512,768]{1,0:T(8,128)(2,1)}, u32[]{:S(2)}) copy-start(bf16[512,768]{1,0:T(8,128)(2,1)} %param.18) | copy-start | bytes 2359300
  225.9 0.9 copy-start.13
  232.1 13.0 %slice-start = ((s8[12582912]{0:T(1024)(128)(4,1)}), s8[4194304]{0:T(1024)(128)(4,1)S(1)}, s32[]{:S(2)}) async-start(s8[12582912]{0:T(1024)(128)(4,1)} %bitcast.123), calls=%async_computation.13 | async-start | bytes 8388608
  234.7 10.4 %slice-start.1 = ((s8[12582912]{0:T(1024)(128)(4,1)}), s8[4194304]{0:T(1024)(128)(4,1)S(1)}, s32[]{:S(2)}) async-start(s8[12582912]{0:T(1024)(128)(4,1)} %bitcast.123), calls=%async_computation.14 | async-start | bytes 8388608
  234.7 11.7 %slice-start.2 = ((s8[12582912]{0:T(1024)(128)(4,1)}), s8[4194304]{0:T(1024)(128)(4,1)S(1)}, s32[]{:S(2)}) async-start(s8[12582912]{0:T(1024)(128)(4,1)} %bitcast.123), calls=%async_computation.15 | async-start | bytes 8388608
  234.7 11.7 %copy-start.22 = (f32[12,512]{1,0:T(8,128)S(1)}, f32[12,512]{1,0:T(8,128)}, u32[]{:S(2)}) copy-start(f32[12,512]{1,0:T(8,128)} %copy-done.21) | copy-start | bytes 73732
  246.4 6.9 %copy-start.18 = (bf16[768,512]{1,0:T(8,128)(2,1)S(1)}, bf16[768,512]{1,0:T(8,128)(2,1)}, u32[]{:S(2)}) copy-start(bf16[768,512]{1,0:T(8,128)(2,1)} %copy-done.17) | copy-start | bytes 2359300
  253.3 2.7 copy-start
  253.3 3.5 copy-start.39
  256.0 0.9 copy-start.15
  262.2 2.5 copy-start.5
  264.7 4.0 copy-start.40
  274.1 1.6 copy-start.1
  274.1 2.0 copy-start.2
  278.6 54.5 %reduce-scatter.21.cloned.1.call-start = ((), (), s32[]{:S(2)}) async-start(), calls=%async_computation.10 | async-start | bytes 2949120
  278.7 12.8 %copy-start.23 = (f32[768]{0:T(1024)S(1)}, f32[768]{0:T(1024)}, u32[]{:S(2)}) copy-start(f32[768]{0:T(1024)} %get-tuple-element.42) | copy-start | bytes 9220
  278.7 12.8 %copy-start.30 = (f32[768]{0:T(1024)S(1)}, f32[768]{0:T(1024)}, u32[]{:S(2)}) copy-start(f32[768]{0:T(1024)} %get-tuple-element.29) | copy-start | bytes 9220
  278.7 12.8 %copy-start.29 = (f32[768]{0:T(1024)S(1)}, f32[768]{0:T(1024)}, u32[]{:S(2)}) copy-start(f32[768]{0:T(1024)} %get-tuple-element.34) | copy-start | bytes 9220
  278.7 12.8 %copy-start.25 = (f32[768]{0:T(1024)S(1)}, f32[768]{0:T(1024)}, u32[]{:S(2)}) copy-start(f32[768]{0:T(1024)} %get-tuple-element.40) | copy-start | bytes 9220
  279.2 94.5 %reduce-scatter.23.cloned.1.call-start = ((), (), s32[]{:S(2)}) async-start(), calls=%async_computation.11 | async-start | bytes 2949120
  279.2 135.2 %copy-start.27 = (f32[12,64]{1,0:T(8,128)S(1)}, f32[12,64]{1,0:T(8,128)}, u32[]{:S(2)}) copy-start(f32[12,64]{1,0:T(8,128)} %get-tuple-element.73) | copy-start | bytes 9220
  279.3 135.3 %copy-start.26 = (f32[3072]{0:T(1024)S(1)}, f32[3072]{0:T(1024)}, u32[]{:S(2)}) copy-start(f32[3072]{0:T(1024)} %get-tuple-element.75) | copy-start | bytes 36868
  279.3 180.4 %copy-start.16 = (bf16[12,64,512]{2,1,0:T(8,128)(2,1)S(1)}, bf16[12,64,512]{2,1,0:T(8,128)(2,1)}, u32[]{:S(2)}) copy-start(bf16[12,64,512]{2,1,0:T(8,128)(2,1)} %copy-done.15) | copy-start | bytes 2359300
  279.8 134.6 %reduce-scatter.19.cloned.1.call-start = ((), (), s32[]{:S(2)}) async-start(), calls=%async_computation.9 | async-start | bytes 2949120
  291.4 203.1 %all-reduce.6.cloned.1.call-start = ((), (), s32[]{:S(2)}) async-start(), calls=%async_computation.12 | async-start | bytes 3538944 | tf_op jit(solution)/shard_map/psum | solution.py:135
  459.0 2.8 copy-start.33
  461.8 1.3 copy-start.9
  461.8 1.6 copy-start.14
  494.5 2.3 copy-start.20
  494.5 3.4 copy-start.19
Sparse Core Ops, SparseCore 0:
  181.3 12.1 reduce-scatter.14
  204.7 12.3 reduce-scatter.16
  278.7 12.5 reduce-scatter.12
  294.6 38.5 reduce-scatter.20
  336.3 37.3 reduce-scatter.22
  376.9 37.3 reduce-scatter.18
  417.1 77.3 all-reduce.5
